TPU v7x, 128 devices: a whole 4x4x4 slice. The times are simulated.
128 devices in a mesh: group: 4 (over x), slab: 32 (over z, y, core).
Axes of the slice: x: 4, y: 4, z: 4, core: 2. Of those that a mesh axis runs over, the one named last changes fastest.
Arguments:
- queries: float32 [512, 1024], P(('group', 'slab')), may hold values from -6 to 6
- probes: int32 [512, 32], P(('group', 'slab')), may hold values from 0 to 511, all different within a row; in each aligned block of 4 rows (0 to 3, 4 to 7, ...) at most 2 rows name the same one
- codes: bfloat16 [512, 2048, 1024], P(('group', 'slab')), may hold values from 0 to 255, as said below
- scale: float32 [512, 1024], P(('group', 'slab')), may hold values from 4e-05 to 0.00032
- offset: float32 [512, 1024], P(('group', 'slab')), may hold values from -0.5 to 0.5
- tile_counts: int32 [512], P(('group', 'slab')), may hold values from 1 to 8, 2304 in all
- raw_vectors: float32 [131072, 1024], P(('group', 'slab')), may hold values from -0.5 to 0.5
- candidates: int32 [512, 64], P(('group', 'slab')), may hold values from 0 to 131071, as said below
Outputs:
- list_best: float32 [512, 32], P(('group', 'slab'))
- rerank: float32 [512, 64], P(('group', 'slab'))
Inputs may be any that keep to these rules, and one draw needn't show every extreme that they name: `probes`: each query names 32 different lists; among the 4 queries of one device no list is named by more than 2 queries. List l is held by device l // 4 in the order of group+slab. `tile_counts`: some list uses all 8 tiles. `codes`: every entry is a whole number, an 8-bit level. `candidates`: vector v is stored on device v // 1024 in the order of group+slab. Among the ids of one device's queries at most 4 lie on any one device, and exactly 4 on some device.
All inputs are finite; a program needn't handle non-finite values. No bound on the sum of `tile_counts` on one device may be relied on, other than what follows from the above.
Results may differ from a plain program's by a relative error of at most 0.0013.
Values sent between devices are 32-bit elements; how exact they have to be, the bound alone decides.
No kernel may reach another device: no remote copies, remote signals or barrier semaphores. Data moves between devices by JAX's collectives and lax.ppermute only.
A program may use at most 128 MiB of HBM per device.

v0:
```python
import jax
import jax.numpy as jnp
from jax import lax
from jax.sharding import PartitionSpec as P

TILE = 256


def send_queries(outgoing):
    return lax.all_to_all(outgoing, ("group", "slab"), split_axis=0, concat_axis=0, tiled=True)


def send_scores(best_found):
    return lax.all_to_all(best_found, ("group", "slab"), split_axis=0, concat_axis=0, tiled=True)


def local(queries, probes, codes, scale, offset, tile_counts, raw_vectors, candidates):
    devices = lax.axis_size("group") * lax.axis_size("slab")
    q_dev, width = queries.shape
    list_dev, slab_rows, _ = codes.shape
    lists = list_dev * devices
    probe_count = probes.shape[1]
    slot_most = max(2, 2 * q_dev * probe_count // lists)
    slot_range = jnp.arange(slot_most, dtype=jnp.int32)
    list_ids = jnp.arange(lists, dtype=jnp.int32)
    hit_table = jnp.any(probes[:, :, None] == list_ids[None, None, :], axis=1).astype(jnp.int32)
    hit_rank = jnp.cumsum(hit_table, axis=0) - hit_table
    select = (hit_table[:, :, None] * (hit_rank[:, :, None] == slot_range[None, None, :])).astype(
        jnp.float32
    )
    outgoing = jnp.einsum("qlm,qd->lmd", select, queries, precision=lax.Precision.HIGHEST)
    arrived = send_queries(outgoing.reshape(devices, list_dev * slot_most, width))
    arrived = arrived.reshape(devices, list_dev, slot_most, width)
    row_ids = jnp.arange(slab_rows, dtype=jnp.int32)
    results = []
    for list_pos in range(list_dev):
        chosen = arrived[:, list_pos].reshape(devices * slot_most, width)
        folded = (chosen * scale[list_pos]).astype(jnp.bfloat16)
        base_score = jnp.dot(chosen, offset[list_pos], precision=lax.Precision.HIGHEST)
        list_codes = codes[list_pos]
        scores = jnp.einsum("qd,rd->qr", folded, list_codes, preferred_element_type=jnp.float32)
        row_valid = row_ids < tile_counts[list_pos] * TILE
        best_score = jnp.max(jnp.where(row_valid[None, :], scores, -1e30), axis=1)
        results.append(best_score + base_score)
    best_found = jnp.stack(results, axis=0).reshape(list_dev, devices, slot_most).transpose(1, 0, 2)
    replies = send_scores(best_found).reshape(lists * slot_most)
    probe_rank = jnp.take_along_axis(hit_rank, probes, axis=1)
    list_best = replies[probes * slot_most + probe_rank]
    cand_count = candidates.shape[1]
    v_dev = raw_vectors.shape[0]
    store_cap = max(2, 2 * q_dev * cand_count // devices)
    flat_ids = candidates.reshape(-1)
    owner_dev = flat_ids // v_dev
    local_row = flat_ids % v_dev
    owner_table = (owner_dev[:, None] == jnp.arange(devices, dtype=jnp.int32)[None, :]).astype(
        jnp.int32
    )
    owner_rank = jnp.take_along_axis(
        jnp.cumsum(owner_table, axis=0) - owner_table, owner_dev[:, None], axis=1
    )[:, 0]
    slot_index = owner_dev * store_cap + owner_rank
    request = (
        jnp.zeros((devices * store_cap,), jnp.int32)
        .at[slot_index]
        .set(local_row)
        .reshape(devices, store_cap)
    )
    asked = lax.all_to_all(request, ("group", "slab"), split_axis=0, concat_axis=0, tiled=True)
    fetched = raw_vectors[asked.reshape(-1)].reshape(devices, store_cap, width)
    vector_back = lax.all_to_all(
        fetched, ("group", "slab"), split_axis=0, concat_axis=0, tiled=True
    )
    vectors = vector_back.reshape(devices * store_cap, width)[slot_index].reshape(
        q_dev, cand_count, width
    )
    rerank = jnp.einsum("qd,qkd->qk", queries, vectors, precision=lax.Precision.HIGHEST)
    return (list_best, rerank)


def solution(mesh):
    in_specs = (
        P(("group", "slab"), None),
        P(("group", "slab"), None),
        P(("group", "slab"), None, None),
        P(("group", "slab"), None),
        P(("group", "slab"), None),
        P(("group", "slab")),
        P(("group", "slab"), None),
        P(("group", "slab"), None),
    )
    out_specs = (P(("group", "slab"), None), P(("group", "slab"), None))
    return jax.shard_map(local, mesh=mesh, in_specs=in_specs, out_specs=out_specs, check_vma=False)
```

profile of v0, /device:TPU:1, one launch (start us, length us, event | category | flops | bytes accessed | tf_op | source)
XLA Modules:
  0.0 200.8 jit_solution(13158260502432270511)
XLA Ops:
  0.6 0.0 copy-start
  0.6 0.8 reshape.392
  1.4 0.8 reshape.394
  2.2 0.8 reshape.395
  2.9 0.8 reshape.391
  3.7 0.1 copy.30
  3.8 0.2 fusion.37
  4.1 0.1 copy.32
  4.3 2.4 %gather_fusion.4 = s32[256]{0:T(256)S(1)} fusion(s32[256,128]{0,1:T(8,128)S(1)} %bitcast_subtract_fusion, s32[256]{0:T(256)S(1)} %bitcast.93), kind=kCustom, calls=%fused_computation.4 | custom fusion | bytes 4096 | tf_op jit(solution)/shard_map/jit(take_along_axis)/gather | solution.py:58
  6.7 1.4 scatter_custom_fusion
  8.1 0.1 all_to_all.17
  8.2 20.8 %all_to_all.24 = s32[128,1,4]{2,1,0:T(1,128)S(1)} all-to-all(s32[128,1,4]{2,1,0:T(1,128)S(1)} %bitcast.98), channel_id=1, replica_groups=mesh['group'=4,'slab'=32] {'group','slab'}, dimensions={0} | all-to-all | bytes 4096 | tf_op jit(solution)/shard_map/all_to_all | solution.py:68
  29.0 0.5 broadcast.494
  29.6 0.8 reduce.3
  30.4 0.1 reshape.396
  30.5 5.0 %gather_fusion.1 = f32[512,1024]{1,0:T(8,128)S(1)} fusion(f32[1024,1024]{1,0:T(8,128)} %param.14, s32[1024]{0:T(1024)S(1)} %pad_clamp_fusion.1), kind=kCustom, calls=%fused_computation.1 | custom fusion | bytes 4196352 | tf_op jit(solution)/shard_map/gather | solution.py:69
  35.5 0.0 copy-start.4
  35.5 1.7 reshape.397
  37.3 4.6 %all-to-all-start.3 = ((f32[128,4,1024]{2,1,0:T(4,128)}), f32[128,4,1024]{2,1,0:T(4,128)S(1)}, u32[]{:S(2)}, u32[]{:S(2)}) async-start(f32[128,4,1024]{2,1,0:T(4,128)} %reshape.397), calls=%async_computation.3 | async-start | bytes 4194304 | tf_op jit(solution)/shard_map/all_to_all | solution.py:70
  41.9 0.0 copy-done.4
  41.9 0.1 fusion.36
  42.1 3.5 %fusion.42 = f32[512,2,1024]{2,0,1:T(8,128)S(1)} fusion(s32[4,512]{1,0:T(4,128)S(1)} %convert_element_type.45, s32[4,512]{1,0:T(4,128)S(1)} %convert_subtract_fusion, f32[4,1024]{1,0:T(4,128)S(1)} %copy-done), kind=kOutput, calls=%fused_computation.42 | convolution fusion | flops 50343936 | bytes 4227072 | tf_op jit(solution)/shard_map/qlm,qd->lmd/dot_general | solution.py:31
  45.6 5.2 %copy.27 = f32[512,2,1024]{2,1,0:T(2,128)} copy(f32[512,2,1024]{2,0,1:T(8,128)S(1)} %fusion.42) | data formatting | bytes 8388608 | tf_op jit(solution)/shard_map/qlm,qd->lmd/dot_general | solution.py:31
  50.8 6.1 %reshape.387 = f32[128,8,1024]{2,1,0:T(8,128)} reshape(f32[512,2,1024]{2,1,0:T(2,128)} %copy.27) | data formatting | bytes 8388608 | tf_op jit(solution)/shard_map/reshape | solution.py:32
  56.8 15.4 %all-to-all-done.3 = f32[128,4,1024]{2,1,0:T(4,128)S(1)} async-done(((f32[128,4,1024]{2,1,0:T(4,128)}), f32[128,4,1024]{2,1,0:T(4,128)S(1)}, u32[]{:S(2)}, u32[]{:S(2)}) %all-to-all-start.3) | async-done | bytes 2097184 | tf_op jit(solution)/shard_map/all_to_all | solution.py:70
  72.3 5.7 %all-to-all-start = ((f32[128,8,1024]{2,1,0:T(8,128)}), f32[128,8,1024]{2,1,0:T(8,128)}, u32[]{:S(2)}, u32[]{:S(2)}) async-start(f32[128,8,1024]{2,1,0:T(8,128)} %reshape.387), calls=%async_computation | async-start | bytes 8388608 | tf_op jit(solution)/shard_map/all_to_all | solution.py:10
  78.0 0.7 fusion.70
  81.2 0.1 reshape.424
  81.3 1.5 gather_fusion.3
  82.8 0.1 reshape.427
  82.9 0.1 reshape.402
  83.1 2.0 reshape.398
  85.1 1.1 gather_fusion.2
  86.2 44.5 %all-to-all-done = f32[128,8,1024]{2,1,0:T(8,128)} async-done(((f32[128,8,1024]{2,1,0:T(8,128)}), f32[128,8,1024]{2,1,0:T(8,128)}, u32[]{:S(2)}, u32[]{:S(2)}) %all-to-all-start) | async-done | bytes 4194336 | tf_op jit(solution)/shard_map/all_to_all | solution.py:10
  130.7 5.8 %reshape.388 = f32[128,4,2,1024]{3,2,1,0:T(2,128)} reshape(f32[128,8,1024]{2,1,0:T(8,128)} %all-to-all-done) | data formatting | bytes 8388608 | tf_op jit(solution)/shard_map/reshape | solution.py:33
  136.5 6.0 %fusion.68 = (f32[128,1,2,1024]{3,2,1,0:T(2,128)}, bf16[128,1,2,1024]{3,2,1,0:T(2,128)(2,1)}, bf16[128,1,2,1024]{3,2,1,0:T(2,128)(2,1)}, bf16[128,1,2,1024]{3,2,...) fusion(f32[128,4,2,1024]{3,2,1,0:T(2,128)} %reshape.388, ...), kind=kLoop, calls=%fused_computation.108 | loop fusion | flops 2097152 | bytes 10502144 | tf_op jit(solution)/shard_map/slice | solution.py:37
  142.5 2.1 %convert_element_type.48 = bf16[256,1024]{1,0:T(8,128)(2,1)} reshape(bf16[128,1,2,1024]{3,2,1,0:T(2,128)(2,1)} %get-tuple-element.3) | data formatting | bytes 1048576 | tf_op jit(solution)/shard_map/convert_element_type | solution.py:38
  144.5 2.9 %reshape_squeeze.12 = f32[256,1024]{1,0:T(8,128)} reshape(f32[128,1,2,1024]{3,2,1,0:T(2,128)} %get-tuple-element.2) | data formatting | bytes 2097152 | tf_op jit(solution)/shard_map/reshape;squeeze | solution.py:37
  147.4 2.1 %fusion.54 = f32[1,256]{1,0:T(1,128)S(1)} fusion(f32[256,1024]{1,0:T(8,128)} %reshape_squeeze.12, f32[4,1024]{1,0:T(4,128)S(1)} %copy-done.3), kind=kOutput, calls=%fused_computation.68 | convolution fusion | flops 3145728 | bytes 1053696 | tf_op jit(solution)/shard_map/dot_general | solution.py:39
  149.6 3.7 %fusion.33 = f32[256]{0:T(256)S(1)} fusion(bf16[256,1024]{1,0:T(8,128)(2,1)} %convert_element_type.48, bf16[4,2048,1024]{2,1,0:T(8,128)(2,1)} %param.10, pred[2048]{0:T(1024)(128)(4,1)S(1)} %iota_compare_fusion.7), kind=kOutput, calls=%fused_computation.25 | convolution fusion | flops 1074790144 | bytes 4721664 | tf_op jit(solution)/shard_map/qd,rd->qr/dot_general | solution.py:41
  153.3 0.1 stack.15
  153.5 2.0 %convert_element_type.50 = bf16[256,1024]{1,0:T(8,128)(2,1)} reshape(bf16[128,1,2,1024]{3,2,1,0:T(2,128)(2,1)} %get-tuple-element.4) | data formatting | bytes 1048576 | tf_op jit(solution)/shard_map/convert_element_type | solution.py:38
  155.5 2.9 %reshape_squeeze.13 = f32[256,1024]{1,0:T(8,128)} reshape(f32[128,1,2,1024]{3,2,1,0:T(2,128)} %get-tuple-element.9) | data formatting | bytes 2097152 | tf_op jit(solution)/shard_map/reshape;squeeze | solution.py:37
  158.5 2.1 %fusion.52 = f32[1,256]{1,0:T(1,128)S(1)} fusion(f32[256,1024]{1,0:T(8,128)} %reshape_squeeze.13, f32[4,1024]{1,0:T(4,128)S(1)} %copy-done.3), kind=kOutput, calls=%fused_computation.66 | convolution fusion | flops 3145728 | bytes 1053696 | tf_op jit(solution)/shard_map/dot_general | solution.py:39
  160.6 3.7 %fusion.30 = f32[256]{0:T(256)S(1)} fusion(bf16[256,1024]{1,0:T(8,128)(2,1)} %convert_element_type.50, bf16[4,2048,1024]{2,1,0:T(8,128)(2,1)} %param.10, pred[2048]{0:T(1024)(128)(4,1)S(1)} %iota_compare_fusion.6), kind=kOutput, calls=%fused_computation.24 | convolution fusion | flops 1074790144 | bytes 4721664 | tf_op jit(solution)/shard_map/qd,rd->qr/dot_general | solution.py:41
  164.4 0.1 stack.16
  164.5 2.1 %convert_element_type.52 = bf16[256,1024]{1,0:T(8,128)(2,1)} reshape(bf16[128,1,2,1024]{3,2,1,0:T(2,128)(2,1)} %get-tuple-element.5) | data formatting | bytes 1048576 | tf_op jit(solution)/shard_map/convert_element_type | solution.py:38
  166.6 1.7 reshape_squeeze.14
  168.3 2.1 %fusion.50 = f32[1,256]{1,0:T(1,128)S(1)} fusion(f32[256,1024]{1,0:T(8,128)} %reshape_squeeze.14, f32[4,1024]{1,0:T(4,128)S(1)} %copy-done.3), kind=kOutput, calls=%fused_computation.64 | convolution fusion | flops 3145728 | bytes 1053696 | tf_op jit(solution)/shard_map/dot_general | solution.py:39
  170.4 3.8 %fusion.27 = f32[256]{0:T(256)S(1)} fusion(bf16[256,1024]{1,0:T(8,128)(2,1)} %convert_element_type.52, bf16[4,2048,1024]{2,1,0:T(8,128)(2,1)} %param.10, pred[2048]{0:T(1024)(128)(4,1)S(1)} %iota_compare_fusion.5), kind=kOutput, calls=%fused_computation.23 | convolution fusion | flops 1074790144 | bytes 4721664 | tf_op jit(solution)/shard_map/qd,rd->qr/dot_general | solution.py:41
  174.2 0.1 stack.17
  174.4 1.0 convert_element_type.54
  175.4 0.7 reshape_squeeze.15
  176.1 0.9 fusion.48
  177.0 3.7 %fusion.24 = f32[256]{0:T(256)S(1)} fusion(bf16[256,1024]{1,0:T(8,128)(2,1)} %convert_element_type.54, bf16[4,2048,1024]{2,1,0:T(8,128)(2,1)} %param.10, pred[2048]{0:T(1024)(128)(4,1)S(1)} %iota_compare_fusion.4), kind=kOutput, calls=%fused_computation.22 | convolution fusion | flops 1074790144 | bytes 4721664 | tf_op jit(solution)/shard_map/qd,rd->qr/dot_general | solution.py:41
  180.7 0.1 stack.18
  180.9 1.5 copy.28
  182.4 5.7 %all-to-all-start.1 = ((f32[128,4,2]{1,2,0:T(2,128)}), f32[128,4,2]{1,2,0:T(2,128)S(1)}, u32[]{:S(2)}, u32[]{:S(2)}) async-start(f32[128,4,2]{1,2,0:T(2,128)} %copy.28), calls=%async_computation.1 | async-start | bytes 262144 | tf_op jit(solution)/shard_map/all_to_all | solution.py:14
  188.1 1.6 fusion.40
  189.7 8.4 %all-to-all-done.1 = f32[128,4,2]{1,2,0:T(2,128)S(1)} async-done(((f32[128,4,2]{1,2,0:T(2,128)}), f32[128,4,2]{1,2,0:T(2,128)S(1)}, u32[]{:S(2)}, u32[]{:S(2)}) %all-to-all-start.1) | async-done | bytes 4128 | tf_op jit(solution)/shard_map/all_to_all | solution.py:14
  198.0 0.9 copy.29
  198.9 0.2 reshape.389
  199.2 1.0 gather_fusion
  200.2 0.7 reshape.401
  (44 shorter events, 0.4 us)
Async XLA Ops:
  0.6 41.4 %copy-start = (f32[4,1024]{1,0:T(4,128)S(1)}, f32[4,1024]{1,0:T(4,128)}, u32[]{:S(2)}) copy-start(f32[4,1024]{1,0:T(4,128)} %param.8) | copy-start | bytes 49156
  35.5 6.4 %copy-start.4 = (s32[4,32]{1,0:T(4,128)S(1)}, s32[4,32]{1,0:T(4,128)}, u32[]{:S(2)}) copy-start(s32[4,32]{1,0:T(4,128)} %param.9) | copy-start | bytes 1540
  37.3 35.0 %all-to-all-start.3 = ((f32[128,4,1024]{2,1,0:T(4,128)}), f32[128,4,1024]{2,1,0:T(4,128)S(1)}, u32[]{:S(2)}, u32[]{:S(2)}) async-start(f32[128,4,1024]{2,1,0:T(4,128)} %reshape.397), calls=%async_computation.3 | async-start | bytes 4194304 | tf_op jit(solution)/shard_map/all_to_all | solution.py:70
  56.8 21.1 %copy-start.6 = (s32[4]{0:T(128)S(1)}, s32[4]{0:T(128)}, u32[]{:S(2)}) copy-start(s32[4]{0:T(128)} %param.13) | copy-start | bytes 52
  56.8 26.2 %copy-start.5 = (f32[4,1024]{1,0:T(4,128)S(1)}, f32[4,1024]{1,0:T(4,128)}, u32[]{:S(2)}) copy-start(f32[4,1024]{1,0:T(4,128)} %param.11) | copy-start | bytes 49156
  72.3 6.4 %copy-start.1 = (f32[128,4,1024]{2,1,0:T(4,128)}, f32[128,4,1024]{2,1,0:T(4,128)S(1)}, u32[]{:S(2)}) copy-start(f32[128,4,1024]{2,1,0:T(4,128)S(1)} %all-to-all-done.3) | copy-start | bytes 6291460
  72.3 58.4 %all-to-all-start = ((f32[128,8,1024]{2,1,0:T(8,128)}), f32[128,8,1024]{2,1,0:T(8,128)}, u32[]{:S(2)}, u32[]{:S(2)}) async-start(f32[128,8,1024]{2,1,0:T(8,128)} %reshape.387), calls=%async_computation | async-start | bytes 8388608 | tf_op jit(solution)/shard_map/all_to_all | solution.py:10
  136.5 11.0 %copy-start.3 = (f32[4,1024]{1,0:T(4,128)S(1)}, f32[4,1024]{1,0:T(4,128)}, u32[]{:S(2)}) copy-start(f32[4,1024]{1,0:T(4,128)} %param.12) | copy-start | bytes 49156
  170.4 4.0 %copy-start.2 = (bf16[128,1,2,1024]{3,2,1,0:T(2,128)(2,1)S(1)}, bf16[128,1,2,1024]{3,2,1,0:T(2,128)(2,1)}, u32[]{:S(2)}) copy-start(bf16[128,1,2,1024]{3,2,1,0:T(2,128)(2,1)} %get-tuple-element.6) | copy-start | bytes 1572868
  182.4 15.6 %all-to-all-start.1 = ((f32[128,4,2]{1,2,0:T(2,128)}), f32[128,4,2]{1,2,0:T(2,128)S(1)}, u32[]{:S(2)}, u32[]{:S(2)}) async-start(f32[128,4,2]{1,2,0:T(2,128)} %copy.28), calls=%async_computation.1 | async-start | bytes 262144 | tf_op jit(solution)/shard_map/all_to_all | solution.py:14
where the time goes:
time: 202 us; the launch traced here: 201 us
  waiting for transfers between devices  68.3 us (34%)
  local copies, waits for them, and re-layouts  57.4 us (28%)
  matrix products  27.4 us (14%)
  blocking collectives  20.8 us (10%)
  starting transfers between devices  16 us (8%)
  other arithmetic  7.41 us (4%)
  between operations  3.55 us (2%)
    all_to_all x1, waiting for transfers between devices, send_queries(): lax.all_to_all(outgoing, ('group', 'slab'), split_axis=0, concat_axis=0,...  44.5 us
    all_to_all x1, blocking collectives, local(): lax.all_to_all(request, ('group', 'slab'), split_axis=0, concat_axis=0, t...  20.8 us
    all_to_all x1, waiting for transfers between devices, local(): lax.all_to_all(fetched, ('group', 'slab'), split_axis=0, concat_axis=0, t...  15.4 us
    dot_general x4, matrix products, local(): jnp.einsum('qd,rd->qr', folded, list_codes, preferred_element_type=jnp.fl...  15 us
    all_to_all x1, waiting for transfers between devices, send_scores(): lax.all_to_all(best_found, ('group', 'slab'), split_axis=0, concat_axis=0...  8.37 us
    another operation x4, local copies, waits for them, and re-layouts, local(): chosen = arrived[:, list_pos].reshape(devices * slot_most, width)  8.29 us
    dot_general x4, matrix products, local(): jnp.dot(chosen, offset[list_pos], precision=lax.Precision.HIGHEST)  7.32 us
    convert_element_type x4, local copies, waits for them, and re-layouts, local(): folded = (chosen * scale[list_pos]).astype(jnp.bfloat16)  7.15 us
  transfers between devices with their start and end apart: 3, of which 3 were waited for; matrix products, arithmetic and copies ran while one was open for 11% of the time, Pallas kernels for 0%

commit v1 on v0

v1 whole, which is shorter than its diff:
```python
import functools

import jax
import jax.numpy as jnp
from jax import lax
from jax.experimental import pallas as pl
from jax.experimental.pallas import tpu as pltpu
from jax.sharding import PartitionSpec as P

TILE = 256
AXES = ("group", "slab")
ROWS = 40
F32 = jnp.float32
BF16 = jnp.bfloat16
HIGH = lax.Precision.HIGHEST
NT = (((1,), (1,)), ((), ()))
NN = (((1,), (0,)), ((), ()))


def dot(a, b, dims=NN, precision=None):
    return lax.dot_general(a, b, dims, precision=precision, preferred_element_type=F32)


def iota(shape, dim):
    return lax.broadcasted_iota(jnp.int32, shape, dim)


def vmem():
    return pl.BlockSpec(memory_space=pltpu.VMEM)


def smem():
    return pl.BlockSpec(memory_space=pltpu.SMEM)


def hbm():
    return pl.BlockSpec(memory_space=pl.ANY)


def pack_kernel(me_ref, q_ref, p_ref, c_ref, out_ref):
    q_dev = q_ref.shape[0]
    for q in range(q_dev):
        for c in range(8):
            out_ref[q * 8 + c : q * 8 + c + 1, :] = q_ref[q : q + 1, c * 128 : (c + 1) * 128]
    probes = p_ref[...].astype(F32)
    out_ref[32:33, :] = jnp.concatenate([probes[q : q + 1, :] for q in range(q_dev)], axis=1)
    cands = c_ref[...].astype(F32)
    out_ref[33:34, :] = jnp.concatenate([cands[0:1, :], cands[1:2, :]], axis=1)
    out_ref[34:35, :] = jnp.concatenate([cands[2:3, :], cands[3:4, :]], axis=1)
    out_ref[35:40, :] = jnp.full((5, 128), me_ref[0], jnp.int32).astype(F32)


def pack(me, queries, probes, candidates):
    return pl.pallas_call(
        pack_kernel,
        out_shape=jax.ShapeDtypeStruct((ROWS, 128), F32),
        in_specs=[smem(), vmem(), vmem(), vmem()],
        out_specs=vmem(),
    )(me, queries, probes, candidates)


def split_kernel(v_ref, hi_ref, lo_ref):
    v = v_ref[...]
    hi = v.astype(BF16)
    hi_ref[...] = hi
    lo_ref[...] = (v - hi.astype(F32)).astype(BF16)


def split(v):
    rows, width = v.shape
    blk = pl.BlockSpec((256, width), lambda i: (i, 0))
    return pl.pallas_call(
        split_kernel,
        grid=(rows // 256,),
        out_shape=[jax.ShapeDtypeStruct(v.shape, BF16)] * 2,
        in_specs=[blk],
        out_specs=[blk, blk],
    )(v)


def score_kernel(
    me_ref, tc_ref, *refs, n_blocks, per_block, n_lists, n_rows
):
    blocks = refs[:n_blocks]
    scale_ref, offset_ref, vhi_ref, vlo_ref, codes_ref, out_ref = refs[n_blocks : n_blocks + 6]
    code_buf, fold, base_acc, qhi, qlo, sems = refs[n_blocks + 6 :]
    me = me_ref[0]
    n_tiles = n_rows // TILE
    dev = n_blocks * per_block

    for l in range(n_lists):
        for t in range(n_tiles):
            pltpu.make_async_copy(
                codes_ref.at[l, pl.ds(t * TILE, TILE), :],
                code_buf.at[l, pl.ds(t * TILE, TILE), :],
                sems.at[l, t],
            ).start()

    def rows_of(r):
        return jnp.concatenate(
            [b[pl.ds(r, per_block, stride=ROWS), :] for b in blocks], axis=0
        )

    probe = rows_of(32)
    eq = jnp.concatenate(
        [(probe == (me * n_lists + l).astype(F32)).astype(BF16) for l in range(n_lists)], axis=0
    )
    seg = (iota((128, 512), 0) // 32 == iota((128, 512), 1) // 128).astype(BF16)
    hits = dot(eq, seg)
    ident = rows_of(35)
    perm = (ident == iota((dev, 128), 1).astype(F32)).astype(F32)

    for b in range(n_blocks):
        for g in range(per_block // 8):
            r0 = b * per_block + g * 8
            q_val = [
                [blocks[b][pl.ds(g * 8 * ROWS + q * 8 + c, 8, stride=ROWS), :] for c in range(8)]
                for q in range(4)
            ]
            for q in range(4):
                for c in range(8):
                    x = q_val[q][c]
                    hi = x.astype(BF16)
                    qhi[q * dev + r0 : q * dev + r0 + 8, c * 128 : (c + 1) * 128] = hi.astype(F32)
                    qlo[q * dev + r0 : q * dev + r0 + 8, c * 128 : (c + 1) * 128] = x - hi.astype(F32)
            for l in range(n_lists):
                h = [hits[l * dev + r0 : l * dev + r0 + 8, q * 128 : (q + 1) * 128] for q in range(3)]
                m0, m1, m2 = h[0] > 0.5, h[1] > 0.5, h[2] > 0.5
                s1 = (h[0] + h[1]) > 1.5
                s2 = (h[0] + h[1] + h[2]) > 1.5
                acc = [None, None]
                for c in range(8):
                    x = [q_val[q][c] for q in range(4)]
                    first = jnp.where(m0, x[0], jnp.where(m1, x[1], jnp.where(m2, x[2], x[3])))
                    second = jnp.where(s1, x[1], jnp.where(s2, x[2], x[3]))
                    sc = scale_ref[l : l + 1, c * 128 : (c + 1) * 128]
                    of = offset_ref[l : l + 1, c * 128 : (c + 1) * 128]
                    for s, pick in enumerate((first, second)):
                        fold[l, s * dev + r0 : s * dev + r0 + 8, c * 128 : (c + 1) * 128] = pick * sc
                        part = pick * of
                        acc[s] = part if acc[s] is None else acc[s] + part
                for s in range(2):
                    base_acc[l, s * dev + r0 : s * dev + r0 + 8, :] = acc[s]

    ones = jnp.ones((8, 128), F32)
    out_rows = []
    for l in range(n_lists):
        folded = fold[l].astype(BF16)
        best = None
        for t in range(n_tiles):
            pltpu.make_async_copy(
                codes_ref.at[l, pl.ds(t * TILE, TILE), :],
                code_buf.at[l, pl.ds(t * TILE, TILE), :],
                sems.at[l, t],
            ).wait()
            s = dot(code_buf[l, t * TILE : (t + 1) * TILE, :], folded, NT)
            m = jnp.max(s.reshape(TILE // 8, 8, 2 * dev), axis=0)
            if t == 0:
                best = m
            else:
                best = jnp.where(t < tc_ref[l], jnp.maximum(best, m), best)
        best = jnp.max(best, axis=0, keepdims=True)
        base = dot(ones, base_acc[l], NT, HIGH)[0:1, :]
        total = best + base
        out_rows += [total[:, :dev], total[:, dev:]]

    cand = jnp.concatenate([rows_of(33), rows_of(34)], axis=1)
    v_dev = vhi_ref.shape[0]
    local_id = cand - (me * v_dev).astype(F32)
    mine = (local_id >= 0.0) & (local_id < float(v_dev))
    tri = (iota((256, 256), 0) < iota((256, 256), 1)).astype(BF16)
    rank = dot(mine.astype(BF16), tri)
    place = local_id + (iota((dev, 256), 1) // 64 * v_dev).astype(F32)
    wide = jnp.ones((256, 128), F32)
    spot = [
        dot(jnp.where(mine & (rank == float(s)), place, 0.0), wide, NN, HIGH) for s in range(4)
    ]
    spot = [(x + 0.5).astype(jnp.int32) for x in spot]
    found = [jnp.zeros((dev, 128), F32) for _ in range(4)]
    for q in range(4):
        hi = qhi[q * dev : (q + 1) * dev, :].astype(BF16)
        lo = qlo[q * dev : (q + 1) * dev, :].astype(BF16)
        for n in range(v_dev // 256):
            vh = vhi_ref[n * 256 : (n + 1) * 256, :]
            vl = vlo_ref[n * 256 : (n + 1) * 256, :]
            s = dot(hi, vh, NT) + dot(lo, vh, NT) + dot(hi, vl, NT)
            for h in range(2):
                lane = iota((dev, 128), 1) + (q * v_dev + n * 256 + h * 128)
                for k in range(4):
                    found[k] = jnp.where(spot[k] == lane, s[:, h * 128 : (h + 1) * 128], found[k])
    for k in range(4):
        out_rows.append(dot(ones, found[k], NT, HIGH)[0:1, :])
    pad = jnp.zeros((16 - len(out_rows), dev), F32)
    table = jnp.concatenate(out_rows + [pad], axis=0)
    table = dot(table, perm, NN, HIGH)
    table = jnp.concatenate([table, jnp.zeros((112, 128), F32)], axis=0)
    out_ref[...] = table.T


def score(me, tile_counts, blocks, scale, offset, vhi, vlo, codes):
    n_lists, n_rows, width = codes.shape
    per_block = blocks[0].shape[0]
    blocks = [b.reshape(per_block * ROWS, 128) for b in blocks]
    dev = per_block * len(blocks)
    return pl.pallas_call(
        functools.partial(
            score_kernel, n_blocks=len(blocks), per_block=per_block, n_lists=n_lists, n_rows=n_rows
        ),
        out_shape=jax.ShapeDtypeStruct((dev, 128), F32),
        in_specs=[smem(), smem()] + [vmem()] * (len(blocks) + 4) + [hbm()],
        out_specs=vmem(),
        scratch_shapes=[
            pltpu.VMEM(codes.shape, BF16),
            pltpu.VMEM((n_lists, 2 * dev, width), F32),
            pltpu.VMEM((n_lists, 2 * dev, 128), F32),
            pltpu.VMEM((4 * dev, width), F32),
            pltpu.VMEM((4 * dev, width), F32),
            pltpu.SemaphoreType.DMA((n_lists, n_rows // TILE)),
        ],
        compiler_params=pltpu.CompilerParams(vmem_limit_bytes=56 * 1024 * 1024),
    )(me, tile_counts, *blocks, scale, offset, vhi, vlo, codes)


def pick_kernel(got_ref, p_ref, c_ref, best_ref, rerank_ref):
    got = got_ref[...].T[0:16, :]
    probes, cands = p_ref[...], c_ref[...]
    name = jnp.concatenate([probes[q : q + 1, :] for q in range(4)], axis=1)
    across = jnp.broadcast_to(name, (128, 128))
    down = across.T
    earlier = iota((128, 128), 0) // 32 < iota((128, 128), 1) // 32
    rank = jnp.sum(jnp.where((down == across) & earlier, 1, 0), axis=0, keepdims=True)
    row_of = (name % 4) * 2 + rank
    pairs = [(name // 4, row_of)]
    ids = [
        jnp.concatenate([cands[0:1, :], cands[1:2, :]], axis=1),
        jnp.concatenate([cands[2:3, :], cands[3:4, :]], axis=1),
    ]
    owner = [x // 1024 for x in ids]
    wide = [jnp.broadcast_to(x, (128, 128)) for x in owner]
    tall = [x.T for x in wide]
    before = iota((128, 128), 0) < iota((128, 128), 1)
    first = jnp.sum(jnp.where((tall[0] == wide[0]) & before, 1, 0), axis=0, keepdims=True)
    second = jnp.sum(jnp.where(tall[0] == wide[1], 1, 0), axis=0, keepdims=True) + jnp.sum(
        jnp.where((tall[1] == wide[1]) & before, 1, 0), axis=0, keepdims=True
    )
    pairs += [(owner[0], 8 + first), (owner[1], 8 + second)]
    vals = []
    for holder, row in pairs:
        hot = (iota((128, 128), 0) == holder).astype(F32)
        w = dot(got, hot, NN, HIGH)
        vals.append(jnp.sum(jnp.where(iota((16, 128), 0) == row, w, 0.0), axis=0, keepdims=True))
    best_ref[...] = jnp.concatenate([vals[0][:, q * 32 : (q + 1) * 32] for q in range(4)], axis=0)
    rerank_ref[...] = jnp.concatenate(
        [vals[1 + q // 2][:, (q % 2) * 64 : (q % 2) * 64 + 64] for q in range(4)], axis=0
    )


def pick(got, probes, candidates):
    return pl.pallas_call(
        pick_kernel,
        out_shape=(
            jax.ShapeDtypeStruct(probes.shape, F32),
            jax.ShapeDtypeStruct(candidates.shape, F32),
        ),
        in_specs=[vmem()] * 3,
        out_specs=(vmem(), vmem()),
    )(got, probes, candidates)


def place_of(x, z, y, c):
    return ((x * 4 + z) * 4 + y) * 2 + c


def shift_pairs(step, axis_of_core):
    pairs = []
    for x in range(4):
        for z in range(4):
            for y in range(4):
                for c in range(2):
                    at = {"x": x, "z": z, "y": y}
                    at[axis_of_core[c]] = (at[axis_of_core[c]] + step) % 4
                    pairs.append((place_of(x, z, y, c), place_of(at["x"], at["z"], at["y"], c)))
    return pairs


def other_core():
    return [(i, i ^ 1) for i in range(128)]


ORDERS = ("xy", "yz", "zx")


def local(queries, probes, codes, scale, offset, tile_counts, raw_vectors, candidates):
    me = lax.axis_index(AXES).astype(jnp.int32).reshape(1)
    packet = pack(me, queries, probes, candidates)
    vhi, vlo = split(raw_vectors)
    have = packet[None]
    for stage in range(2):
        got = [lax.ppermute(have, AXES, shift_pairs(k, ORDERS[stage])) for k in (1, 2, 3)]
        have = jnp.concatenate([have] + got, axis=0)
    blocks = [have] + [lax.ppermute(have, AXES, shift_pairs(k, ORDERS[2])) for k in (1, 3, 2)]
    blocks = blocks + [lax.ppermute(b, AXES, other_core()) for b in blocks]
    found = score(me, tile_counts, blocks, scale, offset, vhi, vlo, codes)
    devices = found.shape[0]
    back = lax.all_to_all(found.reshape(devices, 1, 128), AXES, split_axis=0, concat_axis=0, tiled=True)
    return pick(back.reshape(devices, 128), probes, candidates)


def solution(mesh):
    in_specs = (
        P(AXES, None),
        P(AXES, None),
        P(AXES, None, None),
        P(AXES, None),
        P(AXES, None),
        P(AXES),
        P(AXES, None),
        P(AXES, None),
    )
    out_specs = (P(AXES, None), P(AXES, None))
    return jax.shard_map(local, mesh=mesh, in_specs=in_specs, out_specs=out_specs, check_vma=False)
```

time: 202 us -> 90.2 us (0.45)
  waiting for transfers between devices: 68.3 us -> 7.46 us
  local copies, waits for them, and re-layouts: 57.4 us -> 1.78 us
  Pallas kernels: 0 us -> 38.3 us
  matrix products: 27.4 us -> 0 us
  starting transfers between devices: 16 us -> 25.6 us
  other arithmetic: 7.41 us -> 0.73 us
  blocking collectives: 20.8 us -> 15.1 us
  between operations: 3.55 us -> 0.78 us
    all_to_all x3 -> x0, waiting for transfers between devices: 68.3 us -> none  [the longest x1 44.5 us: send_queries(): lax.all_to_all(outgoing, ('group', 'slab'), split_axis=0, concat_axis=0,...]
    pallas_call x0 -> x4, Pallas kernels: none -> 38.3 us  [the longest x1 30.2 us: score(): pl.pallas_call(functools.partial(score_kernel, n_blocks=len(blocks), per_...]
    dot_general x10 -> x0, matrix products: 27.4 us -> none  [the longest x4 15 us: local(): jnp.einsum('qd,rd->qr', folded, list_codes, preferred_element_type=jnp.fl...]
    ppermute x0 -> x13, starting transfers between devices: none -> 25.6 us  [the longest x4 11.9 us: local(): blocks = blocks + [lax.ppermute(b, AXES, other_core()) for b in blocks]]
    reshape x10 -> x0, local copies, waits for them, and re-layouts: 19 us -> none  [the longest x1 6.05 us: local(): outgoing.reshape(devices, list_dev * slot_most, width)]
    all_to_all x3 -> x0, starting transfers between devices: 16 us -> none  [the longest x1 5.69 us: send_queries(): lax.all_to_all(outgoing, ('group', 'slab'), split_axis=0, concat_axis=0,...]
    gather x8 -> x0, local copies, waits for them, and re-layouts: 11.8 us -> none  [the longest x1 5.01 us: local(): fetched = raw_vectors[asked.reshape(-1)].reshape(devices, store_cap, width)]
    another operation x12 -> x0, local copies, waits for them, and re-layouts: 8.96 us -> none  [the longest x4 8.29 us: local(): chosen = arrived[:, list_pos].reshape(devices * slot_most, width)]
  transfers between devices with their start and end apart: 3 -> 13, of which waited for: 3 -> 3; matrix products, arithmetic and copies ran while one was open for 11% -> 1% of each run, Pallas kernels for 0% -> 5%
where the time goes in v1:
time: 90.2 us; the launch traced here: 89.7 us
  Pallas kernels  38.3 us (42%)
  starting transfers between devices  25.6 us (28%)
  blocking collectives  15.1 us (17%)
  waiting for transfers between devices  7.46 us (8%)
  local copies, waits for them, and re-layouts  1.78 us (2%)
    pallas_call x1, Pallas kernels, score(): pl.pallas_call(functools.partial(score_kernel, n_blocks=len(blocks), per_...  30.2 us
    all_to_all x1, blocking collectives, local(): lax.all_to_all(found.reshape(devices, 1, 128), AXES, split_axis=0, concat...  15.1 us
    ppermute x4, starting transfers between devices, local(): blocks = blocks + [lax.ppermute(b, AXES, other_core()) for b in blocks]  11.9 us
    ppermute x6, starting transfers between devices, local(): lax.ppermute(have, AXES, shift_pairs(k, ORDERS[stage]))  9.06 us
    ppermute x6, waiting for transfers between devices, local(): lax.ppermute(have, AXES, shift_pairs(k, ORDERS[stage]))  7.44 us
    pallas_call x1, Pallas kernels, split(): pl.pallas_call(split_kernel, grid=(rows // 256,), out_shape=[jax.ShapeDty...  4.77 us
    ppermute x3, starting transfers between devices, local(): lax.ppermute(have, AXES, shift_pairs(k, ORDERS[2]))  4.58 us
    pallas_call x1, Pallas kernels, pick(): pl.pallas_call(pick_kernel, out_shape=(jax.ShapeDtypeStruct(probes.shape,...  1.87 us
  transfers between devices with their start and end apart: 13, of which 3 were waited for; matrix products, arithmetic and copies ran while one was open for 1% of the time, Pallas kernels for 5%

profile of v1, /device:TPU:1, one launch (start us, length us, event | category | flops | bytes accessed | tf_op | source)
XLA Modules:
  0.0 89.7 jit_solution(1471569317228424093)
XLA Ops:
  0.6 1.4 %shard_map.95 = f32[40,128]{1,0:T(8,128)} custom-call(s32[1]{0:T(128)} %bitcast.me_ref, f32[4,1024]{1,0:T(4,128)} %q_ref.1, s32[4,32]{1,0:T(4,128)} %p_ref.3, s32[4,64]{1,0:T(4,128)} %c_ref.3), custom_call_target="tpu_custom_call" | custom-call | tf_op jit(solution)/shard_map/pallas_call | solution.py:54
  2.1 3.6 %collective-permute-start.2 = (f32[1,40,128]{2,1,0:T(8,128)}, f32[1,40,128]{2,1,0:T(8,128)S(1)}, u32[]{:S(2)}, u32[]{:S(2)}) collective-permute-start(f32[1,40,128]{2,1,0:T(8,128)} %bitcast.25), channel_id=1, source_target_pairs={{0,96},{1,7},{2,98},{3,1},{4,100},{5,3},{6,102},{7,5},{8,104},{9,1... | collective-permute-start | bytes 61448 | tf_op jit(solution)/shard_map/ppermute | solution.py:299
  5.6 0.3 collective-permute-start.1
  6.0 0.7 collective-permute-start
  6.7 0.8 constant_dynamic-update-slice_fusion.6
  7.4 0.0 collective-permute-done.2
  7.4 2.6 %collective-permute-done.1 = f32[1,40,128]{2,1,0:T(8,128)S(1)} collective-permute-done((f32[1,40,128]{2,1,0:T(8,128)}, f32[1,40,128]{2,1,0:T(8,128)S(1)}, u32[]{:S(2)}, u32[]{:S(2)}) %collective-permute-start.1) | collective-permute-done | bytes 20512 | tf_op jit(solution)/shard_map/ppermute | solution.py:299
  10.0 0.2 collective-permute-done
  10.2 0.7 pad_maximum_fusion
  10.9 3.8 %collective-permute-start.5 = (f32[4,40,128]{2,1,0:T(8,128)S(1)}, f32[4,40,128]{2,1,0:T(8,128)S(1)}, u32[]{:S(2)}, u32[]{:S(2)}) collective-permute-start(f32[4,40,128]{2,1,0:T(8,128)S(1)} %pad_maximum_fusion), channel_id=1, source_target_pairs={{0,6},{1,25},{2,0},{3,27},{4,2},{5,29},{6,4},{7,31},{8,14},{9,1},{... | collective-permute-start | bytes 245768 | tf_op jit(solution)/shard_map/ppermute | solution.py:299
  14.7 0.0 collective-permute-start.4
  14.7 0.7 collective-permute-start.3
  15.4 4.7 %collective-permute-done.3 = f32[4,40,128]{2,1,0:T(8,128)S(1)} collective-permute-done((f32[4,40,128]{2,1,0:T(8,128)S(1)}, f32[4,40,128]{2,1,0:T(8,128)S(1)}, u32[]{:S(2)}, u32[]{:S(2)}) %collective-permute-start.3) | collective-permute-done | bytes 81952 | tf_op jit(solution)/shard_map/ppermute | solution.py:299
  20.1 0.0 collective-permute-done.4
  20.1 0.0 collective-permute-done.5
  20.1 0.0 copy-start
  20.1 3.1 %collective-permute-start.8 = (f32[16,40,128]{2,1,0:T(8,128)S(1)}, f32[16,40,128]{2,1,0:T(8,128)S(1)}, u32[]{:S(2)}, u32[]{:S(2)}) collective-permute-start(f32[16,40,128]{2,1,0:T(8,128)S(1)} %constant_dynamic-update-slice_fusion), channel_id=1, source_target_pairs={{0,16},{1,65},{2,18},{3,67},{4,20},{5,69},{6,22},{7,71},{8,24},{9,... | collective-permute-start | bytes 983048 | tf_op jit(solution)/shard_map/ppermute | solution.py:301
  23.2 0.9 collective-permute-start.7
  24.1 0.6 collective-permute-start.6
  24.7 4.2 %collective-permute-start.9 = (f32[16,40,128]{2,1,0:T(8,128)S(1)}, f32[16,40,128]{2,1,0:T(8,128)S(1)}, u32[]{:S(2)}, u32[]{:S(2)}) collective-permute-start(f32[16,40,128]{2,1,0:T(8,128)S(1)} %constant_dynamic-update-slice_fusion), channel_id=1, source_target_pairs={{0,1},{1,0},{2,3},{3,2},{4,5},{5,4},{6,7},{7,6},{8,9},{9,8},{10,11... | collective-permute-start | bytes 983048 | tf_op jit(solution)/shard_map/ppermute | solution.py:302
  28.9 0.0 collective-permute-done.8
  28.9 0.0 copy-start.1
  28.9 3.0 %collective-permute-start.12 = (f32[16,40,128]{2,1,0:T(8,128)S(1)}, f32[16,40,128]{2,1,0:T(8,128)S(1)}, u32[]{:S(2)}, u32[]{:S(2)}) collective-permute-start(f32[16,40,128]{2,1,0:T(8,128)S(1)} %collective-permute-done.8), channel_id=1, source_target_pairs={{0,1},{1,0},{2,3},{3,2},{4,5},{5,4},{6,7},{7,6},{8,9},{9,8},{10,11... | collective-permute-start | bytes 983048 | tf_op jit(solution)/shard_map/ppermute | solution.py:302
  32.0 0.0 collective-permute-done.7
  32.0 0.0 copy-start.2
  32.0 4.6 %collective-permute-start.11 = (f32[16,40,128]{2,1,0:T(8,128)S(1)}, f32[16,40,128]{2,1,0:T(8,128)S(1)}, u32[]{:S(2)}, u32[]{:S(2)}) collective-permute-start(f32[16,40,128]{2,1,0:T(8,128)S(1)} %collective-permute-done.7), channel_id=1, source_target_pairs={{0,1},{1,0},{2,3},{3,2},{4,5},{5,4},{6,7},{7,6},{8,9},{9,8},{10,11... | collective-permute-start | bytes 983048 | tf_op jit(solution)/shard_map/ppermute | solution.py:302
  36.5 0.0 collective-permute-done.6
  36.5 0.0 copy-start.3
  36.5 0.1 collective-permute-start.10
  36.6 4.8 %shard_map.96 = (bf16[1024,1024]{1,0:T(8,128)(2,1)}, bf16[1024,1024]{1,0:T(8,128)(2,1)}) custom-call(f32[1024,1024]{1,0:T(8,128)} %v_ref.1), custom_call_target="tpu_custom_call" | custom-call | tf_op jit(solution)/shard_map/pallas_call | solution.py:72
  41.4 0.0 collective-permute-done.9
  41.4 0.0 copy-start.4
  41.4 0.0 collective-permute-done.12
  41.4 0.0 copy-start.5
  41.4 0.0 collective-permute-done.11
  41.5 0.0 copy-start.6
  41.5 0.0 collective-permute-done.10
  41.5 0.0 copy-start.7
  41.5 0.0 copy-done
  41.5 0.0 copy-done.1
  41.5 0.0 copy-done.2
  41.5 0.0 copy-done.3
  41.5 0.6 copy-done.4
  42.1 0.1 copy-done.5
  42.3 0.1 copy-done.6
  42.4 0.1 copy-done.7
  42.5 30.2 %shard_map.97 = f32[128,128]{1,0:T(8,128)} custom-call(s32[1]{0:T(128)} %bitcast.me_ref, s32[4]{0:T(128)} %tc_ref.1, f32[640,128]{1,0:T(8,128)} %bitcast.15, f32[640,128]{1,0:T(8,128)} %bitcast.18, f32[640,128]{1,0:T(8,128)} %bitcast.17, f32[640,128]{1,0:T(8,128)} %bitcast.16, f32[640,128]{1,0:T(8,128)} %bitcast.19, f32[640,128]{1,0:T(8,128)} %bitcast.22, ...), custom_call_target="tpu_custom_call" | custom-call | tf_op jit(solution)/shard_map/pallas_call | solution.py:205
  72.7 15.1 %all_to_all.5 = f32[128,1,128]{2,1,0:T(1,128)} all-to-all(f32[128,1,128]{2,1,0:T(1,128)} %bitcast.23), channel_id=1, replica_groups=mesh['group'=4,'slab'=32] {'group','slab'}, dimensions={0} | all-to-all | bytes 131072 | tf_op jit(solution)/shard_map/all_to_all | solution.py:305
  87.9 1.9 %shard_map.98 = (f32[4,32]{1,0:T(4,128)}, f32[4,64]{1,0:T(4,128)}) custom-call(f32[128,128]{1,0:T(8,128)} %bitcast.24, s32[4,32]{1,0:T(4,128)} %p_ref.3, s32[4,64]{1,0:T(4,128)} %c_ref.3), custom_call_target="tpu_custom_call" | custom-call | tf_op jit(solution)/shard_map/pallas_call | solution.py:259
  (6 shorter events, 0.0 us)
Async XLA Ops:
  2.1 5.4 %collective-permute-start.2 = (f32[1,40,128]{2,1,0:T(8,128)}, f32[1,40,128]{2,1,0:T(8,128)S(1)}, u32[]{:S(2)}, u32[]{:S(2)}) collective-permute-start(f32[1,40,128]{2,1,0:T(8,128)} %bitcast.25), channel_id=1, source_target_pairs={{0,96},{1,7},{2,98},{3,1},{4,100},{5,3},{6,102},{7,5},{8,104},{9,1... | collective-permute-start | bytes 61448 | tf_op jit(solution)/shard_map/ppermute | solution.py:299
  5.6 4.4 %collective-permute-start.1 = (f32[1,40,128]{2,1,0:T(8,128)}, f32[1,40,128]{2,1,0:T(8,128)S(1)}, u32[]{:S(2)}, u32[]{:S(2)}) collective-permute-start(f32[1,40,128]{2,1,0:T(8,128)} %bitcast.26), channel_id=1, source_target_pairs={{0,64},{1,5},{2,66},{3,7},{4,68},{5,1},{6,70},{7,3},{8,72},{9,13},... | collective-permute-start | bytes 61448 | tf_op jit(solution)/shard_map/ppermute | solution.py:299
  6.0 4.2 %collective-permute-start = (f32[1,40,128]{2,1,0:T(8,128)}, f32[1,40,128]{2,1,0:T(8,128)S(1)}, u32[]{:S(2)}, u32[]{:S(2)}) collective-permute-start(f32[1,40,128]{2,1,0:T(8,128)} %bitcast.27), channel_id=1, source_target_pairs={{0,32},{1,3},{2,34},{3,5},{4,36},{5,7},{6,38},{7,1},{8,40},{9,11},... | collective-permute-start | bytes 61448 | tf_op jit(solution)/shard_map/ppermute | solution.py:299
  10.9 9.2 %collective-permute-start.5 = (f32[4,40,128]{2,1,0:T(8,128)S(1)}, f32[4,40,128]{2,1,0:T(8,128)S(1)}, u32[]{:S(2)}, u32[]{:S(2)}) collective-permute-start(f32[4,40,128]{2,1,0:T(8,128)S(1)} %pad_maximum_fusion), channel_id=1, source_target_pairs={{0,6},{1,25},{2,0},{3,27},{4,2},{5,29},{6,4},{7,31},{8,14},{9,1},{... | collective-permute-start | bytes 245768 | tf_op jit(solution)/shard_map/ppermute | solution.py:299
  14.7 5.4 %collective-permute-start.4 = (f32[4,40,128]{2,1,0:T(8,128)S(1)}, f32[4,40,128]{2,1,0:T(8,128)S(1)}, u32[]{:S(2)}, u32[]{:S(2)}) collective-permute-start(f32[4,40,128]{2,1,0:T(8,128)S(1)} %pad_maximum_fusion), channel_id=1, source_target_pairs={{0,4},{1,17},{2,6},{3,19},{4,0},{5,21},{6,2},{7,23},{8,12},{9,25},... | collective-permute-start | bytes 245768 | tf_op jit(solution)/shard_map/ppermute | solution.py:299
  14.7 5.4 %collective-permute-start.3 = (f32[4,40,128]{2,1,0:T(8,128)S(1)}, f32[4,40,128]{2,1,0:T(8,128)S(1)}, u32[]{:S(2)}, u32[]{:S(2)}) collective-permute-start(f32[4,40,128]{2,1,0:T(8,128)S(1)} %pad_maximum_fusion), channel_id=1, source_target_pairs={{0,2},{1,9},{2,4},{3,11},{4,6},{5,13},{6,0},{7,15},{8,10},{9,17},{... | collective-permute-start | bytes 245768 | tf_op jit(solution)/shard_map/ppermute | solution.py:299
  20.1 21.4 %copy-start = (f32[16,40,128]{2,1,0:T(8,128)}, f32[16,40,128]{2,1,0:T(8,128)S(1)}, u32[]{:S(2)}) copy-start(f32[16,40,128]{2,1,0:T(8,128)S(1)} %constant_dynamic-update-slice_fusion) | copy-start | bytes 983044
  20.1 8.8 %collective-permute-start.8 = (f32[16,40,128]{2,1,0:T(8,128)S(1)}, f32[16,40,128]{2,1,0:T(8,128)S(1)}, u32[]{:S(2)}, u32[]{:S(2)}) collective-permute-start(f32[16,40,128]{2,1,0:T(8,128)S(1)} %constant_dynamic-update-slice_fusion), channel_id=1, source_target_pairs={{0,16},{1,65},{2,18},{3,67},{4,20},{5,69},{6,22},{7,71},{8,24},{9,... | collective-permute-start | bytes 983048 | tf_op jit(solution)/shard_map/ppermute | solution.py:301
  23.2 8.7 %collective-permute-start.7 = (f32[16,40,128]{2,1,0:T(8,128)S(1)}, f32[16,40,128]{2,1,0:T(8,128)S(1)}, u32[]{:S(2)}, u32[]{:S(2)}) collective-permute-start(f32[16,40,128]{2,1,0:T(8,128)S(1)} %constant_dynamic-update-slice_fusion), channel_id=1, source_target_pairs={{0,24},{1,97},{2,26},{3,99},{4,28},{5,101},{6,30},{7,103},{8,0},{9... | collective-permute-start | bytes 983048 | tf_op jit(solution)/shard_map/ppermute | solution.py:301
  24.1 12.4 %collective-permute-start.6 = (f32[16,40,128]{2,1,0:T(8,128)S(1)}, f32[16,40,128]{2,1,0:T(8,128)S(1)}, u32[]{:S(2)}, u32[]{:S(2)}) collective-permute-start(f32[16,40,128]{2,1,0:T(8,128)S(1)} %constant_dynamic-update-slice_fusion), channel_id=1, source_target_pairs={{0,8},{1,33},{2,10},{3,35},{4,12},{5,37},{6,14},{7,39},{8,16},{9,4... | collective-permute-start | bytes 983048 | tf_op jit(solution)/shard_map/ppermute | solution.py:301
  24.7 16.7 %collective-permute-start.9 = (f32[16,40,128]{2,1,0:T(8,128)S(1)}, f32[16,40,128]{2,1,0:T(8,128)S(1)}, u32[]{:S(2)}, u32[]{:S(2)}) collective-permute-start(f32[16,40,128]{2,1,0:T(8,128)S(1)} %constant_dynamic-update-slice_fusion), channel_id=1, source_target_pairs={{0,1},{1,0},{2,3},{3,2},{4,5},{5,4},{6,7},{7,6},{8,9},{9,8},{10,11... | collective-permute-start | bytes 983048 | tf_op jit(solution)/shard_map/ppermute | solution.py:302
  28.9 12.5 %copy-start.1 = (f32[16,40,128]{2,1,0:T(8,128)}, f32[16,40,128]{2,1,0:T(8,128)S(1)}, u32[]{:S(2)}) copy-start(f32[16,40,128]{2,1,0:T(8,128)S(1)} %collective-permute-done.8) | copy-start | bytes 983044
  28.9 12.5 %collective-permute-start.12 = (f32[16,40,128]{2,1,0:T(8,128)S(1)}, f32[16,40,128]{2,1,0:T(8,128)S(1)}, u32[]{:S(2)}, u32[]{:S(2)}) collective-permute-start(f32[16,40,128]{2,1,0:T(8,128)S(1)} %collective-permute-done.8), channel_id=1, source_target_pairs={{0,1},{1,0},{2,3},{3,2},{4,5},{5,4},{6,7},{7,6},{8,9},{9,8},{10,11... | collective-permute-start | bytes 983048 | tf_op jit(solution)/shard_map/ppermute | solution.py:302
  32.0 9.5 %copy-start.2 = (f32[16,40,128]{2,1,0:T(8,128)}, f32[16,40,128]{2,1,0:T(8,128)S(1)}, u32[]{:S(2)}) copy-start(f32[16,40,128]{2,1,0:T(8,128)S(1)} %collective-permute-done.7) | copy-start | bytes 983044
  32.0 9.5 %collective-permute-start.11 = (f32[16,40,128]{2,1,0:T(8,128)S(1)}, f32[16,40,128]{2,1,0:T(8,128)S(1)}, u32[]{:S(2)}, u32[]{:S(2)}) collective-permute-start(f32[16,40,128]{2,1,0:T(8,128)S(1)} %collective-permute-done.7), channel_id=1, source_target_pairs={{0,1},{1,0},{2,3},{3,2},{4,5},{5,4},{6,7},{7,6},{8,9},{9,8},{10,11... | collective-permute-start | bytes 983048 | tf_op jit(solution)/shard_map/ppermute | solution.py:302
  36.5 5.0 %copy-start.3 = (f32[16,40,128]{2,1,0:T(8,128)}, f32[16,40,128]{2,1,0:T(8,128)S(1)}, u32[]{:S(2)}) copy-start(f32[16,40,128]{2,1,0:T(8,128)S(1)} %collective-permute-done.6) | copy-start | bytes 983044
  36.5 4.9 %collective-permute-start.10 = (f32[16,40,128]{2,1,0:T(8,128)S(1)}, f32[16,40,128]{2,1,0:T(8,128)S(1)}, u32[]{:S(2)}, u32[]{:S(2)}) collective-permute-start(f32[16,40,128]{2,1,0:T(8,128)S(1)} %collective-permute-done.6), channel_id=1, source_target_pairs={{0,1},{1,0},{2,3},{3,2},{4,5},{5,4},{6,7},{7,6},{8,9},{9,8},{10,11... | collective-permute-start | bytes 983048 | tf_op jit(solution)/shard_map/ppermute | solution.py:302
  41.4 0.7 copy-start.4
  41.4 0.8 copy-start.5
  41.5 0.9 %copy-start.6 = (f32[16,40,128]{2,1,0:T(8,128)}, f32[16,40,128]{2,1,0:T(8,128)S(1)}, u32[]{:S(2)}) copy-start(f32[16,40,128]{2,1,0:T(8,128)S(1)} %collective-permute-done.11) | copy-start | bytes 983044
  41.5 1.0 %copy-start.7 = (f32[16,40,128]{2,1,0:T(8,128)}, f32[16,40,128]{2,1,0:T(8,128)S(1)}, u32[]{:S(2)}) copy-start(f32[16,40,128]{2,1,0:T(8,128)S(1)} %collective-permute-done.10) | copy-start | bytes 983044

commit v2 on v1

v2 whole, which is shorter than its diff:
```python
import functools

import jax
import jax.numpy as jnp
from jax import lax
from jax.experimental import pallas as pl
from jax.experimental.pallas import tpu as pltpu
from jax.sharding import Mesh, PartitionSpec as P

TILE = 256
AXIS = "device"
VLIM = 40
ROWS = 40
F32 = jnp.float32
BF16 = jnp.bfloat16
HIGH = lax.Precision.HIGHEST
NT = (((1,), (1,)), ((), ()))
NN = (((1,), (0,)), ((), ()))


def dot(a, b, dims=NN, precision=None):
    return lax.dot_general(a, b, dims, precision=precision, preferred_element_type=F32)


def iota(shape, dim):
    return lax.broadcasted_iota(jnp.int32, shape, dim)


def vmem():
    return pl.BlockSpec(memory_space=pltpu.VMEM)


def smem():
    return pl.BlockSpec(memory_space=pltpu.SMEM)


def in_hbm(x):
    return pltpu.with_memory_space_constraint(x, pltpu.HBM)


def hbm():
    return pl.BlockSpec(memory_space=pl.ANY)


def pack_kernel(me_ref, q_hbm, p_hbm, c_hbm, out_ref, q_ref, p_ref, c_ref, sems):
    pairs = [(q_hbm, q_ref), (p_hbm, p_ref), (c_hbm, c_ref)]
    arrivals = [pltpu.make_async_copy(src, dst, sems.at[i]) for i, (src, dst) in enumerate(pairs)]
    for copy in arrivals:
        copy.start()
    for copy in arrivals:
        copy.wait()
    q_dev = q_ref.shape[0]
    queries = q_ref[...]
    rows = [queries[q : q + 1, c * 128 : (c + 1) * 128] for q in range(q_dev) for c in range(8)]
    probes = p_ref[...].astype(F32)
    rows.append(jnp.concatenate([probes[q : q + 1, :] for q in range(q_dev)], axis=1))
    cands = c_ref[...].astype(F32)
    rows.append(jnp.concatenate([cands[0:1, :], cands[1:2, :]], axis=1))
    rows.append(jnp.concatenate([cands[2:3, :], cands[3:4, :]], axis=1))
    rows.append(jnp.full((ROWS - len(rows), 128), me_ref[0], jnp.int32).astype(F32))
    packet = jnp.concatenate(rows, axis=0)
    for i in range(out_ref.shape[0]):
        out_ref[i] = packet


def pack(me, queries, probes, candidates, copies):
    return pl.pallas_call(
        pack_kernel,
        out_shape=jax.ShapeDtypeStruct((copies, ROWS, 128), F32),
        in_specs=[smem()] + [hbm()] * 3,
        out_specs=vmem(),
        scratch_shapes=[pltpu.VMEM(x.shape, x.dtype) for x in (queries, probes, candidates)]
        + [pltpu.SemaphoreType.DMA((3,))],
        compiler_params=pltpu.CompilerParams(vmem_limit_bytes=8 * 1024 * 1024),
    )(me, *[in_hbm(x) for x in (queries, probes, candidates)])


def score_kernel(me_ref, *refs, n_blocks, n_lists, n_rows, v_dev):
    blocks = refs[:n_blocks]
    tiles_hbm, scale_hbm, offset_hbm, vecs_hbm, codes_hbm, out_ref = refs[n_blocks : n_blocks + 6]
    (
        tiles_ref, scale_ref, offset_ref, codes_ref, vecs_ref,
        fold, base_acc, prod, spot_v, spot_s, sem, small_sems, vec_sems, code_sems,
    ) = refs[n_blocks + 6 :]
    me = me_ref[0]
    code_copies = [
        pltpu.make_async_copy(codes_hbm.at[l], codes_ref.at[l], code_sems.at[l])
        for l in range(n_lists)
    ]
    vec_copies = [
        pltpu.make_async_copy(
            vecs_hbm.at[:, pl.ds(c * 128, 128)], vecs_ref.at[:, c, :], vec_sems.at[c]
        )
        for c in range(8)
    ]
    small_copies = [
        pltpu.make_async_copy(src, dst, small_sems.at[i])
        for i, (src, dst) in enumerate(
            [(scale_hbm, scale_ref), (offset_hbm, offset_ref), (tiles_hbm, tiles_ref)]
        )
    ]
    for copy in small_copies + [code_copies[0]] + vec_copies + code_copies[1:]:
        copy.start()
    n_tiles = n_rows // TILE
    per = blocks[0].shape[0] // ROWS
    dev = n_blocks * per

    def rows_of(r):
        return jnp.concatenate([b[pl.ds(r, per, stride=ROWS), :] for b in blocks], axis=0)

    cand = jnp.concatenate([rows_of(33), rows_of(34)], axis=1).astype(jnp.int32)
    local_id = cand - me * v_dev
    mine = (local_id >= 0) & (local_id < v_dev)
    tri = (iota((256, 256), 0) < iota((256, 256), 1)).astype(BF16)
    rank = dot(mine.astype(BF16), tri)
    place = local_id + iota((dev, 256), 1) // 64 * v_dev
    high = (place // 64).astype(F32)
    low = (place % 64).astype(F32)
    one = jnp.ones((8, 256), BF16)
    spots = []
    for k in range(4):
        here = mine & (rank == float(k))
        hi = dot(one, jnp.where(here, high, 0.0).astype(BF16), NT)
        lo = dot(one, jnp.where(here, low, 0.0).astype(BF16), NT)
        spots.append((hi[0:1, :] * 64.0 + lo[0:1, :]).astype(jnp.int32))
    spot_v[...] = jnp.concatenate(spots + spots, axis=0)
    to_smem = pltpu.make_async_copy(spot_v, spot_s, sem)
    to_smem.start()

    probe = rows_of(32)
    eq = jnp.concatenate(
        [(probe == (me * n_lists + l).astype(F32)).astype(BF16) for l in range(n_lists)], axis=0
    )
    seg = (iota((128, 384), 0) // 32 == iota((128, 384), 1) // 128).astype(BF16)
    hits = dot(eq, seg)
    ident = rows_of(35)
    perm = (ident == iota((dev, 128), 1).astype(F32)).astype(F32)

    for copy in small_copies:
        copy.wait()
    for b in range(n_blocks):
        r0 = b * per
        for l in range(n_lists):
            h = [hits[l * dev + r0 : l * dev + r0 + per, q * 128 : (q + 1) * 128] for q in range(3)]
            m0, m1, m2 = h[0] > 0.5, h[1] > 0.5, h[2] > 0.5
            s1 = (h[0] + h[1]) > 1.5
            s2 = (h[0] + h[1] + h[2]) > 1.5
            acc = [None, None]
            for c in range(8):
                x = [blocks[b][pl.ds(q * 8 + c, per, stride=ROWS), :] for q in range(4)]
                first = jnp.where(m0, x[0], jnp.where(m1, x[1], jnp.where(m2, x[2], x[3])))
                second = jnp.where(s1, x[1], jnp.where(s2, x[2], x[3]))
                sc = scale_ref[l : l + 1, c * 128 : (c + 1) * 128]
                of = offset_ref[l : l + 1, c * 128 : (c + 1) * 128]
                for s, take in enumerate((first, second)):
                    fold[l, s * dev + r0 : s * dev + r0 + per, c * 128 : (c + 1) * 128] = (
                        take * sc
                    ).astype(BF16)
                    part = take * of
                    acc[s] = part if acc[s] is None else acc[s] + part
            for s in range(2):
                base_acc[l, s * dev + r0 : s * dev + r0 + per, :] = acc[s]

    to_smem.wait()
    for copy in vec_copies:
        copy.wait()

    def gather(b):
        for i in range(per):
            for k in range(4):
                at = spot_s[k, b * per + i]
                q = pl.multiple_of(i * ROWS + at // v_dev * 8, 8)
                j = (k * dev + b * per + i) * 8
                prod[j : j + 8, :] = vecs_ref[at % v_dev] * blocks[b][pl.ds(q, 8), :]

    out_rows = []
    steps = n_lists * n_tiles
    done = 0
    for l in range(n_lists):
        folded = fold[l]
        code_copies[l].wait()
        best = None
        for t in range(n_tiles):
            s = dot(codes_ref[l, t * TILE : (t + 1) * TILE, :], folded, NT)
            m = jnp.max(s.reshape(TILE // 8, 8, 2 * dev), axis=0)
            if t == 0:
                best = m
            else:
                best = jnp.where(t < tiles_ref[l], jnp.maximum(best, m), best)
            if (l * n_tiles + t + 1) * n_blocks // steps > done:
                gather(done)
                done += 1
        best = jnp.max(best, axis=0, keepdims=True)
        for s in range(2):
            base = base_acc[l, s * dev : (s + 1) * dev, :].T
            out_rows.append(best[:, s * dev : (s + 1) * dev] + jnp.sum(base, axis=0, keepdims=True))
    for k in range(4):
        total = None
        for c in range(8):
            x = prod[pl.ds(k * dev * 8 + c, dev, stride=8), :]
            total = x if total is None else total + x
        out_rows.append(jnp.sum(total.T, axis=0, keepdims=True))
    pad = jnp.zeros((16 - len(out_rows), dev), F32)
    table = jnp.concatenate(out_rows + [pad], axis=0)
    table = dot(table, perm, NN, HIGH)
    table = jnp.concatenate([table, jnp.zeros((112, 128), F32)], axis=0)
    out_ref[...] = table.T


def score(me, tile_counts, blocks, scale, offset, vectors, codes):
    n_lists, n_rows, width = codes.shape
    v_dev = vectors.shape[0]
    per = blocks[0].shape[0]
    blocks = [b.reshape(per * ROWS, 128) for b in blocks]
    dev = per * len(blocks)
    body = functools.partial(
        score_kernel, n_blocks=len(blocks), n_lists=n_lists, n_rows=n_rows, v_dev=v_dev
    )
    return pl.pallas_call(
        body,
        out_shape=jax.ShapeDtypeStruct((dev, 128), F32),
        in_specs=[smem()] + [vmem()] * len(blocks) + [hbm()] * 5,
        out_specs=vmem(),
        scratch_shapes=[
            pltpu.SMEM(tile_counts.shape, jnp.int32),
            pltpu.VMEM(scale.shape, F32),
            pltpu.VMEM(offset.shape, F32),
            pltpu.VMEM(codes.shape, BF16),
            pltpu.VMEM((v_dev, 8, 128), F32),
            pltpu.VMEM((n_lists, 2 * dev, width), BF16),
            pltpu.VMEM((n_lists, 2 * dev, 128), F32),
            pltpu.VMEM((4 * dev * 8, 128), F32),
            pltpu.VMEM((8, dev), jnp.int32),
            pltpu.SMEM((8, dev), jnp.int32),
            pltpu.SemaphoreType.DMA,
            pltpu.SemaphoreType.DMA((3,)),
            pltpu.SemaphoreType.DMA((8,)),
            pltpu.SemaphoreType.DMA((n_lists,)),
        ],
        compiler_params=pltpu.CompilerParams(vmem_limit_bytes=VLIM * 1024 * 1024),
    )(
        me, *blocks, *[in_hbm(x) for x in (tile_counts, scale, offset, vectors, codes)]
    )


def pick_kernel(got_ref, p_ref, c_ref, best_ref, rerank_ref):
    got = got_ref[...].T[0:16, :]
    probes, cands = p_ref[...], c_ref[...]
    name = jnp.concatenate([probes[q : q + 1, :] for q in range(4)], axis=1)
    across = jnp.broadcast_to(name, (128, 128))
    down = across.T
    earlier = iota((128, 128), 0) // 32 < iota((128, 128), 1) // 32
    rank = jnp.sum(jnp.where((down == across) & earlier, 1, 0), axis=0, keepdims=True)
    row_of = (name % 4) * 2 + rank
    pairs = [(name // 4, row_of)]
    ids = [
        jnp.concatenate([cands[0:1, :], cands[1:2, :]], axis=1),
        jnp.concatenate([cands[2:3, :], cands[3:4, :]], axis=1),
    ]
    owner = [x // 1024 for x in ids]
    wide = [jnp.broadcast_to(x, (128, 128)) for x in owner]
    tall = [x.T for x in wide]
    before = iota((128, 128), 0) < iota((128, 128), 1)
    first = jnp.sum(jnp.where((tall[0] == wide[0]) & before, 1, 0), axis=0, keepdims=True)
    second = jnp.sum(jnp.where(tall[0] == wide[1], 1, 0), axis=0, keepdims=True) + jnp.sum(
        jnp.where((tall[1] == wide[1]) & before, 1, 0), axis=0, keepdims=True
    )
    pairs += [(owner[0], 8 + first), (owner[1], 8 + second)]
    vals = []
    for holder, row in pairs:
        hot = (iota((128, 128), 0) == holder).astype(F32)
        w = dot(got, hot, NN, HIGH)
        vals.append(jnp.sum(jnp.where(iota((16, 128), 0) == row, w, 0.0), axis=0, keepdims=True))
    best_ref[...] = jnp.concatenate([vals[0][:, q * 32 : (q + 1) * 32] for q in range(4)], axis=0)
    rerank_ref[...] = jnp.concatenate(
        [vals[1 + q // 2][:, (q % 2) * 64 : (q % 2) * 64 + 64] for q in range(4)], axis=0
    )


def pick(got, probes, candidates):
    return pl.pallas_call(
        pick_kernel,
        out_shape=(
            jax.ShapeDtypeStruct(probes.shape, F32),
            jax.ShapeDtypeStruct(candidates.shape, F32),
        ),
        in_specs=[vmem()] * 3,
        out_specs=(vmem(), vmem()),
        compiler_params=pltpu.CompilerParams(vmem_limit_bytes=8 * 1024 * 1024),
    )(got, probes, candidates)


def place_of(at, core):
    return ((at["x"] * 4 + at["z"]) * 4 + at["y"]) * 2 + core


def chips():
    return [{"x": x, "z": z, "y": y} for x in range(4) for z in range(4) for y in range(4)]


def plane_groups(last):
    return [
        [place_of(at, core) for at in chips() if at[last[core]] == place]
        for core in range(2)
        for place in range(4)
    ]


def shift_pairs(step, last):
    pairs = []
    for at in chips():
        for core in range(2):
            to = dict(at)
            to[last[core]] = (at[last[core]] + step) % 4
            pairs.append((place_of(at, core), place_of(to, core)))
    return pairs


def other_core():
    return [(i, i ^ 1) for i in range(128)]


LAST = "zy"


def local(queries, probes, codes, scale, offset, tile_counts, raw_vectors, candidates):
    me = lax.axis_index(AXIS).astype(jnp.int32).reshape(1)
    copies = pack(me, queries, probes, candidates, 16)
    have = lax.all_to_all(
        copies, AXIS, split_axis=0, concat_axis=0, tiled=True, axis_index_groups=plane_groups(LAST)
    )
    blocks = [have] + [lax.ppermute(have, AXIS, shift_pairs(k, LAST)) for k in (1, 3, 2)]
    blocks = blocks + [lax.ppermute(b, AXIS, other_core()) for b in blocks]
    found = score(me, tile_counts, blocks, scale, offset, raw_vectors, codes)
    devices = found.shape[0]
    back = lax.all_to_all(found.reshape(devices, 1, 128), AXIS, split_axis=0, concat_axis=0, tiled=True)
    return pick(back.reshape(devices, 128), probes, candidates)


def solution(mesh):
    flat = Mesh(mesh.devices.reshape(-1), (AXIS,))
    in_specs = (
        P(AXIS, None),
        P(AXIS, None),
        P(AXIS, None, None),
        P(AXIS, None),
        P(AXIS, None),
        P(AXIS),
        P(AXIS, None),
        P(AXIS, None),
    )
    out_specs = (P(AXIS, None), P(AXIS, None))
    return jax.shard_map(local, mesh=flat, in_specs=in_specs, out_specs=out_specs, check_vma=False)
```

time: 90.2 us -> 60.7 us (0.67)
  Pallas kernels: 38.3 us -> 12.3 us
  blocking collectives: 15.1 us -> 30.9 us
  starting transfers between devices: 25.6 us -> 14.1 us
  waiting for transfers between devices: 7.46 us -> 2.45 us
  local copies, waits for them, and re-layouts: 1.78 us -> 0.01 us
    pallas_call x3 -> x2, Pallas kernels: 36.4 us -> 11.3 us  [the longest x1 10.5 us: score(): pl.pallas_call(body, out_shape=jax.ShapeDtypeStruct((dev, 128), F32), in_...]
    all_to_all x1 -> x2, blocking collectives: 15.1 us -> 30.9 us  [the longest x1 16 us: local(): lax.all_to_all(copies, AXIS, split_axis=0, concat_axis=0, tiled=True, axi...]
    ppermute x13 -> x7, starting transfers between devices: 25.6 us -> 14.1 us  [the longest x4 9.77 us: local(): blocks = blocks + [lax.ppermute(b, AXIS, other_core()) for b in blocks]]
    ppermute x13 -> x7, waiting for transfers between devices: 7.46 us -> 2.45 us  [the longest x4 1.55 us: local(): blocks = blocks + [lax.ppermute(b, AXIS, other_core()) for b in blocks]]
    unnamed x22 -> x4, local copies, waits for them, and re-layouts: 1.77 us -> 0.01 us
  transfers between devices with their start and end apart: 13 -> 7, of which waited for: 3 -> 4; matrix products, arithmetic and copies ran while one was open for 1% -> 0% of each run, Pallas kernels for 5% -> 0%
where the time goes in v2:
time: 60.7 us; the launch traced here: 60.4 us
  blocking collectives  30.9 us (51%)
  starting transfers between devices  14.1 us (23%)
  Pallas kernels  12.3 us (20%)
  waiting for transfers between devices  2.45 us (4%)
  between operations  0.68 us (1%)
    all_to_all x1, blocking collectives, local(): lax.all_to_all(copies, AXIS, split_axis=0, concat_axis=0, tiled=True, axi...  16 us
    all_to_all x1, blocking collectives, local(): lax.all_to_all(found.reshape(devices, 1, 128), AXIS, split_axis=0, concat...  14.9 us
    pallas_call x1, Pallas kernels, score(): pl.pallas_call(body, out_shape=jax.ShapeDtypeStruct((dev, 128), F32), in_...  10.5 us
    ppermute x4, starting transfers between devices, local(): blocks = blocks + [lax.ppermute(b, AXIS, other_core()) for b in blocks]  9.77 us
    ppermute x3, starting transfers between devices, local(): lax.ppermute(have, AXIS, shift_pairs(k, LAST))  4.3 us
    ppermute x4, waiting for transfers between devices, local(): blocks = blocks + [lax.ppermute(b, AXIS, other_core()) for b in blocks]  1.55 us
  transfers between devices with their start and end apart: 7, of which 4 were waited for; matrix products, arithmetic and copies ran while one was open for 0% of the time, Pallas kernels for 0%

profile of v2, /device:TPU:1, one launch (start us, length us, event | category | flops | bytes accessed | tf_op | source)
XLA Modules:
  0.0 60.4 jit_solution(8709309241717406953)
XLA Ops:
  0.6 0.0 copy-start.1
  0.6 0.0 copy-start
  0.7 0.8 %shard_map.95 = f32[16,40,128]{2,1,0:T(8,128)S(1)} custom-call(s32[1]{0:T(128)} %bitcast.me_ref, f32[4,1024]{1,0:T(4,128)} %q_hbm.1, s32[4,32]{1,0:T(4,128)} %p_ref.1, s32[4,64]{1,0:T(4,128)} %c_ref.1), custom_call_target="tpu_custom_call" | custom-call | tf_op jit(solution)/shard_map/pallas_call | solution.py:67
  1.5 16.0 %all_to_all.10 = f32[16,40,128]{2,1,0:T(8,128)S(1)} all-to-all(f32[16,40,128]{2,1,0:T(8,128)S(1)} %shard_map.95), channel_id=1, replica_groups={{0,2,4,6,32,34,36,38,64,66,68,70,96,98,100,102},{8,10,12,14,40,42,44,46..., dimensions={0} | all-to-all | bytes 655360 | tf_op jit(solution)/shard_map/all_to_all | solution.py:329
  17.5 2.8 %collective-permute-start.2 = (f32[16,40,128]{2,1,0:T(8,128)S(1)}, f32[16,40,128]{2,1,0:T(8,128)S(1)}, u32[]{:S(2)}, u32[]{:S(2)}) collective-permute-start(f32[16,40,128]{2,1,0:T(8,128)S(1)} %all_to_all.10), channel_id=1, source_target_pairs={{0,16},{1,5},{2,18},{3,7},{4,20},{5,1},{6,22},{7,3},{8,24},{9,13},... | collective-permute-start | bytes 983048 | tf_op jit(solution)/shard_map/ppermute | solution.py:332
  20.3 0.8 %collective-permute-start.1 = (f32[16,40,128]{2,1,0:T(8,128)S(1)}, f32[16,40,128]{2,1,0:T(8,128)S(1)}, u32[]{:S(2)}, u32[]{:S(2)}) collective-permute-start(f32[16,40,128]{2,1,0:T(8,128)S(1)} %all_to_all.10), channel_id=1, source_target_pairs={{0,24},{1,7},{2,26},{3,1},{4,28},{5,3},{6,30},{7,5},{8,0},{9,15},{... | collective-permute-start | bytes 983048 | tf_op jit(solution)/shard_map/ppermute | solution.py:332
  21.1 0.7 %collective-permute-start = (f32[16,40,128]{2,1,0:T(8,128)S(1)}, f32[16,40,128]{2,1,0:T(8,128)S(1)}, u32[]{:S(2)}, u32[]{:S(2)}) collective-permute-start(f32[16,40,128]{2,1,0:T(8,128)S(1)} %all_to_all.10), channel_id=1, source_target_pairs={{0,8},{1,3},{2,10},{3,5},{4,12},{5,7},{6,14},{7,1},{8,16},{9,11},{... | collective-permute-start | bytes 983048 | tf_op jit(solution)/shard_map/ppermute | solution.py:332
  21.8 3.3 %collective-permute-start.3 = (f32[16,40,128]{2,1,0:T(8,128)S(1)}, f32[16,40,128]{2,1,0:T(8,128)S(1)}, u32[]{:S(2)}, u32[]{:S(2)}) collective-permute-start(f32[16,40,128]{2,1,0:T(8,128)S(1)} %all_to_all.10), channel_id=1, source_target_pairs={{0,1},{1,0},{2,3},{3,2},{4,5},{5,4},{6,7},{7,6},{8,9},{9,8},{10,11... | collective-permute-start | bytes 983048 | tf_op jit(solution)/shard_map/ppermute | solution.py:333
  25.1 0.1 collective-permute-done.2
  25.2 3.1 %collective-permute-start.6 = (f32[16,40,128]{2,1,0:T(8,128)S(1)}, f32[16,40,128]{2,1,0:T(8,128)S(1)}, u32[]{:S(2)}, u32[]{:S(2)}) collective-permute-start(f32[16,40,128]{2,1,0:T(8,128)S(1)} %collective-permute-done.2), channel_id=1, source_target_pairs={{0,1},{1,0},{2,3},{3,2},{4,5},{5,4},{6,7},{7,6},{8,9},{9,8},{10,11... | collective-permute-start | bytes 983048 | tf_op jit(solution)/shard_map/ppermute | solution.py:333
  28.3 0.8 %collective-permute-done.1 = f32[16,40,128]{2,1,0:T(8,128)S(1)} collective-permute-done((f32[16,40,128]{2,1,0:T(8,128)S(1)}, f32[16,40,128]{2,1,0:T(8,128)S(1)}, u32[]{:S(2)}, u32[]{:S(2)}) %collective-permute-start.1) | collective-permute-done | bytes 327712 | tf_op jit(solution)/shard_map/ppermute | solution.py:332
  29.1 3.2 %collective-permute-start.5 = (f32[16,40,128]{2,1,0:T(8,128)S(1)}, f32[16,40,128]{2,1,0:T(8,128)S(1)}, u32[]{:S(2)}, u32[]{:S(2)}) collective-permute-start(f32[16,40,128]{2,1,0:T(8,128)S(1)} %collective-permute-done.1), channel_id=1, source_target_pairs={{0,1},{1,0},{2,3},{3,2},{4,5},{5,4},{6,7},{7,6},{8,9},{9,8},{10,11... | collective-permute-start | bytes 983048 | tf_op jit(solution)/shard_map/ppermute | solution.py:333
  32.3 0.0 collective-permute-done
  32.3 0.2 collective-permute-start.4
  32.5 0.0 collective-permute-done.3
  32.5 0.0 collective-permute-done.6
  32.5 1.1 %collective-permute-done.5 = f32[16,40,128]{2,1,0:T(8,128)S(1)} collective-permute-done((f32[16,40,128]{2,1,0:T(8,128)S(1)}, f32[16,40,128]{2,1,0:T(8,128)S(1)}, u32[]{:S(2)}, u32[]{:S(2)}) %collective-permute-start.5) | collective-permute-done | bytes 327712 | tf_op jit(solution)/shard_map/ppermute | solution.py:333
  33.5 0.5 collective-permute-done.4
  34.0 10.5 %shard_map.96 = f32[128,128]{1,0:T(8,128)S(1)} custom-call(s32[1]{0:T(128)} %bitcast.me_ref, f32[640,128]{1,0:T(8,128)S(1)} %bitcast.13, f32[640,128]{1,0:T(8,128)S(1)} %bitcast.16, f32[640,128]{1,0:T(8,128)S(1)} %bitcast.15, f32[640,128]{1,0:T(8,128)S(1)} %bitcast.14, f32[640,128]{1,0:T(8,128)S(1)} %bitcast.17, f32[640,128]{1,0:T(8,128)S(1)} %bitcast.20, ...), custom_call_target="tpu_custom_call" | custom-call | tf_op jit(solution)/shard_map/pallas_call | solution.py:219
  44.5 14.9 %all_to_all.11 = f32[128,1,128]{2,1,0:T(1,128)S(1)} all-to-all(f32[128,1,128]{2,1,0:T(1,128)S(1)} %bitcast.21), channel_id=1, replica_groups=mesh['group'=4,'slab'=32] {'group','slab'}, dimensions={0} | all-to-all | bytes 131072 | tf_op jit(solution)/shard_map/all_to_all | solution.py:336
  59.4 0.0 copy-done.1
  59.4 0.0 copy-done
  59.4 1.0 %shard_map.97 = (f32[4,32]{1,0:T(4,128)}, f32[4,64]{1,0:T(4,128)}) custom-call(f32[128,128]{1,0:T(8,128)S(1)} %bitcast.22, s32[4,32]{1,0:T(4,128)S(1)} %copy-done, s32[4,64]{1,0:T(4,128)S(1)} %copy-done.1), custom_call_target="tpu_custom_call" | custom-call | tf_op jit(solution)/shard_map/pallas_call | solution.py:281
Async XLA Ops:
  0.6 58.8 %copy-start.1 = (s32[4,64]{1,0:T(4,128)S(1)}, s32[4,64]{1,0:T(4,128)}, u32[]{:S(2)}) copy-start(s32[4,64]{1,0:T(4,128)} %c_ref.1) | copy-start | bytes 3076
  0.6 58.8 %copy-start = (s32[4,32]{1,0:T(4,128)S(1)}, s32[4,32]{1,0:T(4,128)}, u32[]{:S(2)}) copy-start(s32[4,32]{1,0:T(4,128)} %p_ref.1) | copy-start | bytes 1540
  17.5 7.7 %collective-permute-start.2 = (f32[16,40,128]{2,1,0:T(8,128)S(1)}, f32[16,40,128]{2,1,0:T(8,128)S(1)}, u32[]{:S(2)}, u32[]{:S(2)}) collective-permute-start(f32[16,40,128]{2,1,0:T(8,128)S(1)} %all_to_all.10), channel_id=1, source_target_pairs={{0,16},{1,5},{2,18},{3,7},{4,20},{5,1},{6,22},{7,3},{8,24},{9,13},... | collective-permute-start | bytes 983048 | tf_op jit(solution)/shard_map/ppermute | solution.py:332
  20.3 8.8 %collective-permute-start.1 = (f32[16,40,128]{2,1,0:T(8,128)S(1)}, f32[16,40,128]{2,1,0:T(8,128)S(1)}, u32[]{:S(2)}, u32[]{:S(2)}) collective-permute-start(f32[16,40,128]{2,1,0:T(8,128)S(1)} %all_to_all.10), channel_id=1, source_target_pairs={{0,24},{1,7},{2,26},{3,1},{4,28},{5,3},{6,30},{7,5},{8,0},{9,15},{... | collective-permute-start | bytes 983048 | tf_op jit(solution)/shard_map/ppermute | solution.py:332
  21.1 11.2 %collective-permute-start = (f32[16,40,128]{2,1,0:T(8,128)S(1)}, f32[16,40,128]{2,1,0:T(8,128)S(1)}, u32[]{:S(2)}, u32[]{:S(2)}) collective-permute-start(f32[16,40,128]{2,1,0:T(8,128)S(1)} %all_to_all.10), channel_id=1, source_target_pairs={{0,8},{1,3},{2,10},{3,5},{4,12},{5,7},{6,14},{7,1},{8,16},{9,11},{... | collective-permute-start | bytes 983048 | tf_op jit(solution)/shard_map/ppermute | solution.py:332
  21.8 10.7 %collective-permute-start.3 = (f32[16,40,128]{2,1,0:T(8,128)S(1)}, f32[16,40,128]{2,1,0:T(8,128)S(1)}, u32[]{:S(2)}, u32[]{:S(2)}) collective-permute-start(f32[16,40,128]{2,1,0:T(8,128)S(1)} %all_to_all.10), channel_id=1, source_target_pairs={{0,1},{1,0},{2,3},{3,2},{4,5},{5,4},{6,7},{7,6},{8,9},{9,8},{10,11... | collective-permute-start | bytes 983048 | tf_op jit(solution)/shard_map/ppermute | solution.py:333
  25.2 7.3 %collective-permute-start.6 = (f32[16,40,128]{2,1,0:T(8,128)S(1)}, f32[16,40,128]{2,1,0:T(8,128)S(1)}, u32[]{:S(2)}, u32[]{:S(2)}) collective-permute-start(f32[16,40,128]{2,1,0:T(8,128)S(1)} %collective-permute-done.2), channel_id=1, source_target_pairs={{0,1},{1,0},{2,3},{3,2},{4,5},{5,4},{6,7},{7,6},{8,9},{9,8},{10,11... | collective-permute-start | bytes 983048 | tf_op jit(solution)/shard_map/ppermute | solution.py:333
  29.1 4.4 %collective-permute-start.5 = (f32[16,40,128]{2,1,0:T(8,128)S(1)}, f32[16,40,128]{2,1,0:T(8,128)S(1)}, u32[]{:S(2)}, u32[]{:S(2)}) collective-permute-start(f32[16,40,128]{2,1,0:T(8,128)S(1)} %collective-permute-done.1), channel_id=1, source_target_pairs={{0,1},{1,0},{2,3},{3,2},{4,5},{5,4},{6,7},{7,6},{8,9},{9,8},{10,11... | collective-permute-start | bytes 983048 | tf_op jit(solution)/shard_map/ppermute | solution.py:333
  32.3 1.7 %collective-permute-start.4 = (f32[16,40,128]{2,1,0:T(8,128)S(1)}, f32[16,40,128]{2,1,0:T(8,128)S(1)}, u32[]{:S(2)}, u32[]{:S(2)}) collective-permute-start(f32[16,40,128]{2,1,0:T(8,128)S(1)} %collective-permute-done), channel_id=1, source_target_pairs={{0,1},{1,0},{2,3},{3,2},{4,5},{5,4},{6,7},{7,6},{8,9},{9,8},{10,11... | collective-permute-start | bytes 983048 | tf_op jit(solution)/shard_map/ppermute | solution.py:333

commit v3 on v2

--- a/solution.py
+++ b/solution.py
@@ -9,7 +9,7 @@
 
 TILE = 256
 AXIS = "device"
-VLIM = 40
+VLIM = 28
 ROWS = 40
 F32 = jnp.float32
 BF16 = jnp.bfloat16
@@ -24,6 +24,16 @@
 
 def iota(shape, dim):
     return lax.broadcasted_iota(jnp.int32, shape, dim)
+
+
+def choose(values, hot):
+    high = values.astype(BF16)
+    rest = values - high.astype(F32)
+    mid = rest.astype(BF16)
+    low = (rest - mid.astype(F32)).astype(BF16)
+    n = values.shape[0]
+    out = dot(jnp.concatenate([high, mid, low], axis=0), hot)
+    return out[:n] + out[n : 2 * n] + out[2 * n :]
 
 
 def vmem():
@@ -75,23 +85,48 @@
     )(me, *[in_hbm(x) for x in (queries, probes, candidates)])
 
 
+def fetch_kernel(have_ref, vecs_ref, have_out, vecs_out, sems):
+    copies = [
+        pltpu.make_async_copy(
+            vecs_ref.at[:, pl.ds(c * 128, 128)], vecs_out.at[:, c, :], sems.at[c]
+        )
+        for c in range(8)
+    ]
+    for copy in copies:
+        copy.start()
+    have_out[...] = have_ref[...]
+    for copy in copies:
+        copy.wait()
+
+
+def fetch(have, vectors):
+    return pl.pallas_call(
+        fetch_kernel,
+        out_shape=(
+            jax.ShapeDtypeStruct(have.shape, F32),
+            pltpu.VMEM((vectors.shape[0], 8, 128), F32),
+        ),
+        in_specs=[vmem(), hbm()],
+        out_specs=(vmem(), vmem()),
+        scratch_shapes=[pltpu.SemaphoreType.DMA((8,))],
+        compiler_params=pltpu.CompilerParams(vmem_limit_bytes=2 * 1024 * 1024),
+        cost_estimate=pl.CostEstimate(
+            flops=0, transcendentals=0, bytes_accessed=2 * vectors.size * 4
+        ),
+    )(have, in_hbm(vectors))
+
+
 def score_kernel(me_ref, *refs, n_blocks, n_lists, n_rows, v_dev):
     blocks = refs[:n_blocks]
-    tiles_hbm, scale_hbm, offset_hbm, vecs_hbm, codes_hbm, out_ref = refs[n_blocks : n_blocks + 6]
+    tiles_hbm, scale_hbm, offset_hbm, vecs_ref, codes_hbm, out_ref = refs[n_blocks : n_blocks + 6]
     (
-        tiles_ref, scale_ref, offset_ref, codes_ref, vecs_ref,
-        fold, base_acc, prod, spot_v, spot_s, sem, small_sems, vec_sems, code_sems,
+        tiles_ref, scale_ref, offset_ref, codes_ref,
+        fold, base_acc, prod, spot_v, spot_s, sem, small_sems, code_sems,
     ) = refs[n_blocks + 6 :]
     me = me_ref[0]
     code_copies = [
         pltpu.make_async_copy(codes_hbm.at[l], codes_ref.at[l], code_sems.at[l])
         for l in range(n_lists)
-    ]
-    vec_copies = [
-        pltpu.make_async_copy(
-            vecs_hbm.at[:, pl.ds(c * 128, 128)], vecs_ref.at[:, c, :], vec_sems.at[c]
-        )
-        for c in range(8)
     ]
     small_copies = [
         pltpu.make_async_copy(src, dst, small_sems.at[i])
@@ -99,7 +134,7 @@
             [(scale_hbm, scale_ref), (offset_hbm, offset_ref), (tiles_hbm, tiles_ref)]
         )
     ]
-    for copy in small_copies + [code_copies[0]] + vec_copies + code_copies[1:]:
+    for copy in small_copies + code_copies[:1]:
         copy.start()
     n_tiles = n_rows // TILE
     per = blocks[0].shape[0] // ROWS
@@ -123,7 +158,10 @@
         hi = dot(one, jnp.where(here, high, 0.0).astype(BF16), NT)
         lo = dot(one, jnp.where(here, low, 0.0).astype(BF16), NT)
         spots.append((hi[0:1, :] * 64.0 + lo[0:1, :]).astype(jnp.int32))
-    spot_v[...] = jnp.concatenate(spots + spots, axis=0)
+    first_row = iota((1, dev), 1) % per * ROWS
+    spot_v[...] = jnp.concatenate(
+        [x % v_dev for x in spots] + [x // v_dev * 8 + first_row for x in spots], axis=0
+    )
     to_smem = pltpu.make_async_copy(spot_v, spot_s, sem)
     to_smem.start()
 
@@ -134,12 +172,15 @@
     seg = (iota((128, 384), 0) // 32 == iota((128, 384), 1) // 128).astype(BF16)
     hits = dot(eq, seg)
     ident = rows_of(35)
-    perm = (ident == iota((dev, 128), 1).astype(F32)).astype(F32)
+    perm = (ident == iota((dev, 128), 1).astype(F32)).astype(BF16)
 
     for copy in small_copies:
         copy.wait()
+    code_copies[1].start()
     for b in range(n_blocks):
         r0 = b * per
+        if b == 4:
+            code_copies[2].start()
         for l in range(n_lists):
             h = [hits[l * dev + r0 : l * dev + r0 + per, q * 128 : (q + 1) * 128] for q in range(3)]
             m0, m1, m2 = h[0] > 0.5, h[1] > 0.5, h[2] > 0.5
@@ -162,16 +203,15 @@
                 base_acc[l, s * dev + r0 : s * dev + r0 + per, :] = acc[s]
 
     to_smem.wait()
-    for copy in vec_copies:
-        copy.wait()
-
-    def gather(b):
-        for i in range(per):
+    code_copies[3].start()
+
+    def gather(part):
+        for j in range(part * 4, part * 4 + 4):
+            b = j // per
             for k in range(4):
-                at = spot_s[k, b * per + i]
-                q = pl.multiple_of(i * ROWS + at // v_dev * 8, 8)
-                j = (k * dev + b * per + i) * 8
-                prod[j : j + 8, :] = vecs_ref[at % v_dev] * blocks[b][pl.ds(q, 8), :]
+                row, q = spot_s[k, j], pl.multiple_of(spot_s[4 + k, j], 8)
+                to = (k * dev + j) * 8
+                prod[to : to + 8, :] = vecs_ref[row] * blocks[b][pl.ds(q, 8), :]
 
     out_rows = []
     steps = n_lists * n_tiles
@@ -187,7 +227,7 @@
                 best = m
             else:
                 best = jnp.where(t < tiles_ref[l], jnp.maximum(best, m), best)
-            if (l * n_tiles + t + 1) * n_blocks // steps > done:
+            if (l * n_tiles + t + 1) * (dev // 4) // steps > done:
                 gather(done)
                 done += 1
         best = jnp.max(best, axis=0, keepdims=True)
@@ -202,7 +242,7 @@
         out_rows.append(jnp.sum(total.T, axis=0, keepdims=True))
     pad = jnp.zeros((16 - len(out_rows), dev), F32)
     table = jnp.concatenate(out_rows + [pad], axis=0)
-    table = dot(table, perm, NN, HIGH)
+    table = choose(table, perm)
     table = jnp.concatenate([table, jnp.zeros((112, 128), F32)], axis=0)
     out_ref[...] = table.T
 
@@ -219,14 +259,13 @@
     return pl.pallas_call(
         body,
         out_shape=jax.ShapeDtypeStruct((dev, 128), F32),
-        in_specs=[smem()] + [vmem()] * len(blocks) + [hbm()] * 5,
+        in_specs=[smem()] + [vmem()] * len(blocks) + [hbm()] * 3 + [vmem(), hbm()],
         out_specs=vmem(),
         scratch_shapes=[
             pltpu.SMEM(tile_counts.shape, jnp.int32),
             pltpu.VMEM(scale.shape, F32),
             pltpu.VMEM(offset.shape, F32),
             pltpu.VMEM(codes.shape, BF16),
-            pltpu.VMEM((v_dev, 8, 128), F32),
             pltpu.VMEM((n_lists, 2 * dev, width), BF16),
             pltpu.VMEM((n_lists, 2 * dev, 128), F32),
             pltpu.VMEM((4 * dev * 8, 128), F32),
@@ -234,25 +273,21 @@
             pltpu.SMEM((8, dev), jnp.int32),
             pltpu.SemaphoreType.DMA,
             pltpu.SemaphoreType.DMA((3,)),
-            pltpu.SemaphoreType.DMA((8,)),
             pltpu.SemaphoreType.DMA((n_lists,)),
         ],
         compiler_params=pltpu.CompilerParams(vmem_limit_bytes=VLIM * 1024 * 1024),
     )(
-        me, *blocks, *[in_hbm(x) for x in (tile_counts, scale, offset, vectors, codes)]
-    )
-
-
-def pick_kernel(got_ref, p_ref, c_ref, best_ref, rerank_ref):
-    got = got_ref[...].T[0:16, :]
+        me, *blocks, *[in_hbm(x) for x in (tile_counts, scale, offset)], vectors, in_hbm(codes)
+    )
+
+
+def where_kernel(p_ref, c_ref, hot_ref, row_ref):
     probes, cands = p_ref[...], c_ref[...]
     name = jnp.concatenate([probes[q : q + 1, :] for q in range(4)], axis=1)
     across = jnp.broadcast_to(name, (128, 128))
-    down = across.T
     earlier = iota((128, 128), 0) // 32 < iota((128, 128), 1) // 32
-    rank = jnp.sum(jnp.where((down == across) & earlier, 1, 0), axis=0, keepdims=True)
-    row_of = (name % 4) * 2 + rank
-    pairs = [(name // 4, row_of)]
+    rank = jnp.sum(jnp.where((across.T == across) & earlier, 1, 0), axis=0, keepdims=True)
+    pairs = [(name // 4, (name % 4) * 2 + rank)]
     ids = [
         jnp.concatenate([cands[0:1, :], cands[1:2, :]], axis=1),
         jnp.concatenate([cands[2:3, :], cands[3:4, :]], axis=1),
@@ -266,18 +301,36 @@
         jnp.where((tall[1] == wide[1]) & before, 1, 0), axis=0, keepdims=True
     )
     pairs += [(owner[0], 8 + first), (owner[1], 8 + second)]
-    vals = []
-    for holder, row in pairs:
-        hot = (iota((128, 128), 0) == holder).astype(F32)
-        w = dot(got, hot, NN, HIGH)
-        vals.append(jnp.sum(jnp.where(iota((16, 128), 0) == row, w, 0.0), axis=0, keepdims=True))
-    best_ref[...] = jnp.concatenate([vals[0][:, q * 32 : (q + 1) * 32] for q in range(4)], axis=0)
+    for i, (holder, row) in enumerate(pairs):
+        hot_ref[:, i * 128 : (i + 1) * 128] = (iota((128, 128), 0) == holder).astype(BF16)
+        row_ref[:, i * 128 : (i + 1) * 128] = jnp.broadcast_to(row, (8, 128))
+
+
+def where_to_look(probes, candidates):
+    return pl.pallas_call(
+        where_kernel,
+        out_shape=(
+            jax.ShapeDtypeStruct((128, 384), BF16),
+            jax.ShapeDtypeStruct((8, 384), jnp.int32),
+        ),
+        in_specs=[vmem()] * 2,
+        out_specs=(vmem(), vmem()),
+        compiler_params=pltpu.CompilerParams(vmem_limit_bytes=4 * 1024 * 1024),
+    )(probes, candidates)
+
+
+def pick_kernel(got_ref, hot_ref, row_ref, best_ref, rerank_ref):
+    got = got_ref[...].T[0:16, :]
+    found = choose(got, hot_ref[...])
+    mask = iota((16, 384), 0) == jnp.concatenate([row_ref[...], row_ref[...]], axis=0)
+    vals = jnp.sum(jnp.where(mask, found, 0.0), axis=0, keepdims=True)
+    best_ref[...] = jnp.concatenate([vals[:, q * 32 : (q + 1) * 32] for q in range(4)], axis=0)
     rerank_ref[...] = jnp.concatenate(
-        [vals[1 + q // 2][:, (q % 2) * 64 : (q % 2) * 64 + 64] for q in range(4)], axis=0
-    )
-
-
-def pick(got, probes, candidates):
+        [vals[:, 128 + q * 64 : 192 + q * 64] for q in range(4)], axis=0
+    )
+
+
+def pick(got, hot, row, probes, candidates):
     return pl.pallas_call(
         pick_kernel,
         out_shape=(
@@ -286,8 +339,8 @@
         ),
         in_specs=[vmem()] * 3,
         out_specs=(vmem(), vmem()),
-        compiler_params=pltpu.CompilerParams(vmem_limit_bytes=8 * 1024 * 1024),
-    )(got, probes, candidates)
+        compiler_params=pltpu.CompilerParams(vmem_limit_bytes=4 * 1024 * 1024),
+    )(got, hot, row)
 
 
 def place_of(at, core):
@@ -330,11 +383,13 @@
         copies, AXIS, split_axis=0, concat_axis=0, tiled=True, axis_index_groups=plane_groups(LAST)
     )
     blocks = [have] + [lax.ppermute(have, AXIS, shift_pairs(k, LAST)) for k in (1, 3, 2)]
-    blocks = blocks + [lax.ppermute(b, AXIS, other_core()) for b in blocks]
-    found = score(me, tile_counts, blocks, scale, offset, raw_vectors, codes)
+    ours, vecs_in = fetch(have, raw_vectors)
+    blocks = blocks + [lax.ppermute(b, AXIS, other_core()) for b in [ours] + blocks[1:]]
+    found = score(me, tile_counts, blocks, scale, offset, vecs_in, codes)
     devices = found.shape[0]
     back = lax.all_to_all(found.reshape(devices, 1, 128), AXIS, split_axis=0, concat_axis=0, tiled=True)
-    return pick(back.reshape(devices, 128), probes, candidates)
+    hot, row = where_to_look(probes, candidates)
+    return pick(back.reshape(devices, 128), hot, row, probes, candidates)
 
 
 def solution(mesh):

time: 60.7 us -> 59.8 us (0.985)
  blocking collectives: 30.9 us -> 16 us
  waiting for transfers between devices: 2.45 us -> 11.6 us
  starting transfers between devices: 14.1 us -> 17.8 us
  Pallas kernels: 12.3 us -> 13.4 us
    all_to_all x1 -> x0, blocking collectives: 14.9 us -> none  [local(): lax.all_to_all(found.reshape(devices, 1, 128), AXIS, split_axis=0, concat...]
    all_to_all x0 -> x1, waiting for transfers between devices: none -> 9.26 us  [local(): lax.all_to_all(found.reshape(devices, 1, 128), AXIS, split_axis=0, concat...]
    all_to_all x0 -> x1, starting transfers between devices: none -> 5.82 us  [local(): lax.all_to_all(found.reshape(devices, 1, 128), AXIS, split_axis=0, concat...]
    pallas_call x0 -> x2, Pallas kernels: none -> 2.51 us  [the longest x1 2.29 us: fetch(): pl.pallas_call(fetch_kernel, out_shape=(jax.ShapeDtypeStruct(have.shape,...]
    ppermute x4, starting transfers between devices: 9.77 us -> 7.66 us  [local(): lax.ppermute(b, AXIS, other_core())]
    pallas_call x1, Pallas kernels: 10.5 us -> 9.24 us  [score(): pl.pallas_call(body, out_shape=jax.ShapeDtypeStruct((dev, 128), F32), in_...]
  transfers between devices with their start and end apart: 7 -> 8, of which waited for: 4 -> 3; matrix products, arithmetic and copies ran while one was open for 0% -> 0% of each run, Pallas kernels for 0% -> 4%
where the time goes in v3:
time: 59.8 us; the launch traced here: 59.5 us
  starting transfers between devices  17.8 us (30%)
  blocking collectives  16 us (27%)
  Pallas kernels  13.4 us (22%)
  waiting for transfers between devices  11.6 us (19%)
  between operations  0.69 us (1%)
    all_to_all x1, blocking collectives, local(): lax.all_to_all(copies, AXIS, split_axis=0, concat_axis=0, tiled=True, axi...  16 us
    all_to_all x1, waiting for transfers between devices, local(): lax.all_to_all(found.reshape(devices, 1, 128), AXIS, split_axis=0, concat...  9.26 us
    pallas_call x1, Pallas kernels, score(): pl.pallas_call(body, out_shape=jax.ShapeDtypeStruct((dev, 128), F32), in_...  9.24 us
    ppermute x4, starting transfers between devices, local(): lax.ppermute(b, AXIS, other_core())  7.66 us
    all_to_all x1, starting transfers between devices, local(): lax.all_to_all(found.reshape(devices, 1, 128), AXIS, split_axis=0, concat...  5.82 us
    ppermute x3, starting transfers between devices, local(): lax.ppermute(have, AXIS, shift_pairs(k, LAST))  4.3 us
    pallas_call x1, Pallas kernels, fetch(): pl.pallas_call(fetch_kernel, out_shape=(jax.ShapeDtypeStruct(have.shape,...  2.29 us
    ppermute x4, waiting for transfers between devices, local(): lax.ppermute(b, AXIS, other_core())  1.25 us
  transfers between devices with their start and end apart: 8, of which 3 were waited for; matrix products, arithmetic and copies ran while one was open for 0% of the time, Pallas kernels for 4%

profile of v3, /device:TPU:1, one launch (start us, length us, event | category | flops | bytes accessed | tf_op | source)
XLA Modules:
  0.0 59.5 jit_solution(12155710675941461122)
XLA Ops:
  0.6 0.8 %shard_map.95 = f32[16,40,128]{2,1,0:T(8,128)S(1)} custom-call(s32[1]{0:T(128)} %bitcast.me_ref, f32[4,1024]{1,0:T(4,128)} %q_hbm.1, s32[4,32]{1,0:T(4,128)} %p_ref.1, s32[4,64]{1,0:T(4,128)} %c_ref.1), custom_call_target="tpu_custom_call" | custom-call | tf_op jit(solution)/shard_map/pallas_call | solution.py:77
  1.5 16.0 %all_to_all.10.have_ref = f32[16,40,128]{2,1,0:T(8,128)S(1)} all-to-all(f32[16,40,128]{2,1,0:T(8,128)S(1)} %shard_map.95), channel_id=1, replica_groups={{0,2,4,6,32,34,36,38,64,66,68,70,96,98,100,102},{8,10,12,14,40,42,44,46..., dimensions={0} | all-to-all | bytes 655360 | tf_op jit(solution)/shard_map/all_to_all | solution.py:382
  17.4 1.2 %collective-permute-start = (f32[16,40,128]{2,1,0:T(8,128)S(1)}, f32[16,40,128]{2,1,0:T(8,128)S(1)}, u32[]{:S(2)}, u32[]{:S(2)}) collective-permute-start(f32[16,40,128]{2,1,0:T(8,128)S(1)} %all_to_all.10.have_ref), channel_id=1, source_target_pairs={{0,8},{1,3},{2,10},{3,5},{4,12},{5,7},{6,14},{7,1},{8,16},{9,11},{... | collective-permute-start | bytes 983048 | tf_op jit(solution)/shard_map/ppermute | solution.py:385
  18.7 1.5 %collective-permute-start.1 = (f32[16,40,128]{2,1,0:T(8,128)S(1)}, f32[16,40,128]{2,1,0:T(8,128)S(1)}, u32[]{:S(2)}, u32[]{:S(2)}) collective-permute-start(f32[16,40,128]{2,1,0:T(8,128)S(1)} %all_to_all.10.have_ref), channel_id=1, source_target_pairs={{0,24},{1,7},{2,26},{3,1},{4,28},{5,3},{6,30},{7,5},{8,0},{9,15},{... | collective-permute-start | bytes 983048 | tf_op jit(solution)/shard_map/ppermute | solution.py:385
  20.2 1.6 %collective-permute-start.2 = (f32[16,40,128]{2,1,0:T(8,128)S(1)}, f32[16,40,128]{2,1,0:T(8,128)S(1)}, u32[]{:S(2)}, u32[]{:S(2)}) collective-permute-start(f32[16,40,128]{2,1,0:T(8,128)S(1)} %all_to_all.10.have_ref), channel_id=1, source_target_pairs={{0,16},{1,5},{2,18},{3,7},{4,20},{5,1},{6,22},{7,3},{8,24},{9,13},... | collective-permute-start | bytes 983048 | tf_op jit(solution)/shard_map/ppermute | solution.py:385
  21.8 2.3 %shard_map.96 = (f32[16,40,128]{2,1,0:T(8,128)S(1)}, f32[1024,8,128]{2,1,0:T(8,128)S(1)}) custom-call(f32[16,40,128]{2,1,0:T(8,128)S(1)} %all_to_all.10.have_ref, f32[1024,1024]{1,0:T(8,128)} %vecs_ref.1), custom_call_target="tpu_custom_call" | custom-call | bytes 8388608 | tf_op jit(solution)/shard_map/pallas_call | solution.py:103
  24.0 3.4 %collective-permute-start.3 = (f32[16,40,128]{2,1,0:T(8,128)S(1)}, f32[16,40,128]{2,1,0:T(8,128)S(1)}, u32[]{:S(2)}, u32[]{:S(2)}) collective-permute-start(f32[16,40,128]{2,1,0:T(8,128)S(1)} %get-tuple-element.6), channel_id=1, source_target_pairs={{0,1},{1,0},{2,3},{3,2},{4,5},{5,4},{6,7},{7,6},{8,9},{9,8},{10,11... | collective-permute-start | bytes 983048 | tf_op jit(solution)/shard_map/ppermute | solution.py:387
  27.4 0.0 collective-permute-done
  27.4 0.6 collective-permute-start.4
  28.0 0.0 collective-permute-done.1
  28.0 0.5 collective-permute-start.5
  28.5 1.1 %collective-permute-done.2 = f32[16,40,128]{2,1,0:T(8,128)S(1)} collective-permute-done((f32[16,40,128]{2,1,0:T(8,128)S(1)}, f32[16,40,128]{2,1,0:T(8,128)S(1)}, u32[]{:S(2)}, u32[]{:S(2)}) %collective-permute-start.2) | collective-permute-done | bytes 327712 | tf_op jit(solution)/shard_map/ppermute | solution.py:385
  29.6 3.2 %collective-permute-start.6 = (f32[16,40,128]{2,1,0:T(8,128)S(1)}, f32[16,40,128]{2,1,0:T(8,128)S(1)}, u32[]{:S(2)}, u32[]{:S(2)}) collective-permute-start(f32[16,40,128]{2,1,0:T(8,128)S(1)} %collective-permute-done.2), channel_id=1, source_target_pairs={{0,1},{1,0},{2,3},{3,2},{4,5},{5,4},{6,7},{7,6},{8,9},{9,8},{10,11... | collective-permute-start | bytes 983048 | tf_op jit(solution)/shard_map/ppermute | solution.py:387
  32.8 0.0 collective-permute-done.3
  32.8 0.0 collective-permute-done.4
  32.8 0.0 collective-permute-done.5
  32.8 1.2 %collective-permute-done.6 = f32[16,40,128]{2,1,0:T(8,128)S(1)} collective-permute-done((f32[16,40,128]{2,1,0:T(8,128)S(1)}, f32[16,40,128]{2,1,0:T(8,128)S(1)}, u32[]{:S(2)}, u32[]{:S(2)}) %collective-permute-start.6) | collective-permute-done | bytes 327712 | tf_op jit(solution)/shard_map/ppermute | solution.py:387
  34.1 0.0 copy-start
  34.1 0.0 copy-start.1
  34.1 9.2 %shard_map.97 = f32[128,128]{1,0:T(8,128)} custom-call(s32[1]{0:T(128)} %bitcast.me_ref, f32[640,128]{1,0:T(8,128)S(1)} %bitcast.13, f32[640,128]{1,0:T(8,128)S(1)} %bitcast.14, f32[640,128]{1,0:T(8,128)S(1)} %bitcast.15, f32[640,128]{1,0:T(8,128)S(1)} %bitcast.16, f32[640,128]{1,0:T(8,128)S(1)} %bitcast.17, f32[640,128]{1,0:T(8,128)S(1)} %bitcast.18, ...), custom_call_target="tpu_custom_call" | custom-call | tf_op jit(solution)/shard_map/pallas_call | solution.py:259
  43.3 5.8 %all-to-all-start.1 = ((f32[128,1,128]{2,1,0:T(1,128)}), f32[128,1,128]{2,1,0:T(1,128)S(1)}, u32[]{:S(2)}, u32[]{:S(2)}) async-start(f32[128,1,128]{2,1,0:T(1,128)} %bitcast.10), calls=%async_computation.1 | async-start | bytes 131072 | tf_op jit(solution)/shard_map/all_to_all | solution.py:390
  49.1 0.0 copy-done
  49.2 0.0 copy-done.1
  49.2 0.2 shard_map.98
  49.4 9.3 %all-to-all-done.1 = f32[128,1,128]{2,1,0:T(1,128)S(1)} async-done(((f32[128,1,128]{2,1,0:T(1,128)}), f32[128,1,128]{2,1,0:T(1,128)S(1)}, u32[]{:S(2)}, u32[]{:S(2)}) %all-to-all-start.1) | async-done | bytes 65568 | tf_op jit(solution)/shard_map/all_to_all | solution.py:390
  58.6 0.9 %shard_map.99 = (f32[4,32]{1,0:T(4,128)}, f32[4,64]{1,0:T(4,128)}) custom-call(f32[128,128]{1,0:T(8,128)S(1)} %bitcast.21, bf16[128,384]{1,0:T(8,128)(2,1)S(1)} %get-tuple-element.8.hot_ref, s32[8,384]{1,0:T(8,128)S(1)} %get-tuple-element.9.row_ref), custom_call_target="tpu_custom_call" | custom-call | tf_op jit(solution)/shard_map/pallas_call | solution.py:334
Async XLA Ops:
  17.4 10.0 %collective-permute-start = (f32[16,40,128]{2,1,0:T(8,128)S(1)}, f32[16,40,128]{2,1,0:T(8,128)S(1)}, u32[]{:S(2)}, u32[]{:S(2)}) collective-permute-start(f32[16,40,128]{2,1,0:T(8,128)S(1)} %all_to_all.10.have_ref), channel_id=1, source_target_pairs={{0,8},{1,3},{2,10},{3,5},{4,12},{5,7},{6,14},{7,1},{8,16},{9,11},{... | collective-permute-start | bytes 983048 | tf_op jit(solution)/shard_map/ppermute | solution.py:385
  18.7 9.3 %collective-permute-start.1 = (f32[16,40,128]{2,1,0:T(8,128)S(1)}, f32[16,40,128]{2,1,0:T(8,128)S(1)}, u32[]{:S(2)}, u32[]{:S(2)}) collective-permute-start(f32[16,40,128]{2,1,0:T(8,128)S(1)} %all_to_all.10.have_ref), channel_id=1, source_target_pairs={{0,24},{1,7},{2,26},{3,1},{4,28},{5,3},{6,30},{7,5},{8,0},{9,15},{... | collective-permute-start | bytes 983048 | tf_op jit(solution)/shard_map/ppermute | solution.py:385
  20.2 9.4 %collective-permute-start.2 = (f32[16,40,128]{2,1,0:T(8,128)S(1)}, f32[16,40,128]{2,1,0:T(8,128)S(1)}, u32[]{:S(2)}, u32[]{:S(2)}) collective-permute-start(f32[16,40,128]{2,1,0:T(8,128)S(1)} %all_to_all.10.have_ref), channel_id=1, source_target_pairs={{0,16},{1,5},{2,18},{3,7},{4,20},{5,1},{6,22},{7,3},{8,24},{9,13},... | collective-permute-start | bytes 983048 | tf_op jit(solution)/shard_map/ppermute | solution.py:385
  24.0 8.8 %collective-permute-start.3 = (f32[16,40,128]{2,1,0:T(8,128)S(1)}, f32[16,40,128]{2,1,0:T(8,128)S(1)}, u32[]{:S(2)}, u32[]{:S(2)}) collective-permute-start(f32[16,40,128]{2,1,0:T(8,128)S(1)} %get-tuple-element.6), channel_id=1, source_target_pairs={{0,1},{1,0},{2,3},{3,2},{4,5},{5,4},{6,7},{7,6},{8,9},{9,8},{10,11... | collective-permute-start | bytes 983048 | tf_op jit(solution)/shard_map/ppermute | solution.py:387
  27.4 5.4 %collective-permute-start.4 = (f32[16,40,128]{2,1,0:T(8,128)S(1)}, f32[16,40,128]{2,1,0:T(8,128)S(1)}, u32[]{:S(2)}, u32[]{:S(2)}) collective-permute-start(f32[16,40,128]{2,1,0:T(8,128)S(1)} %collective-permute-done), channel_id=1, source_target_pairs={{0,1},{1,0},{2,3},{3,2},{4,5},{5,4},{6,7},{7,6},{8,9},{9,8},{10,11... | collective-permute-start | bytes 983048 | tf_op jit(solution)/shard_map/ppermute | solution.py:387
  28.0 4.8 %collective-permute-start.5 = (f32[16,40,128]{2,1,0:T(8,128)S(1)}, f32[16,40,128]{2,1,0:T(8,128)S(1)}, u32[]{:S(2)}, u32[]{:S(2)}) collective-permute-start(f32[16,40,128]{2,1,0:T(8,128)S(1)} %collective-permute-done.1), channel_id=1, source_target_pairs={{0,1},{1,0},{2,3},{3,2},{4,5},{5,4},{6,7},{7,6},{8,9},{9,8},{10,11... | collective-permute-start | bytes 983048 | tf_op jit(solution)/shard_map/ppermute | solution.py:387
  29.6 4.4 %collective-permute-start.6 = (f32[16,40,128]{2,1,0:T(8,128)S(1)}, f32[16,40,128]{2,1,0:T(8,128)S(1)}, u32[]{:S(2)}, u32[]{:S(2)}) collective-permute-start(f32[16,40,128]{2,1,0:T(8,128)S(1)} %collective-permute-done.2), channel_id=1, source_target_pairs={{0,1},{1,0},{2,3},{3,2},{4,5},{5,4},{6,7},{7,6},{8,9},{9,8},{10,11... | collective-permute-start | bytes 983048 | tf_op jit(solution)/shard_map/ppermute | solution.py:387
  34.1 15.1 %copy-start = (s32[4,32]{1,0:T(4,128)S(1)}, s32[4,32]{1,0:T(4,128)}, u32[]{:S(2)}) copy-start(s32[4,32]{1,0:T(4,128)} %p_ref.1) | copy-start | bytes 1540
  34.1 15.1 %copy-start.1 = (s32[4,64]{1,0:T(4,128)S(1)}, s32[4,64]{1,0:T(4,128)}, u32[]{:S(2)}) copy-start(s32[4,64]{1,0:T(4,128)} %c_ref.1) | copy-start | bytes 3076
  43.3 15.3 %all-to-all-start.1 = ((f32[128,1,128]{2,1,0:T(1,128)}), f32[128,1,128]{2,1,0:T(1,128)S(1)}, u32[]{:S(2)}, u32[]{:S(2)}) async-start(f32[128,1,128]{2,1,0:T(1,128)} %bitcast.10), calls=%async_computation.1 | async-start | bytes 131072 | tf_op jit(solution)/shard_map/all_to_all | solution.py:390

commit v4 on v3

--- a/solution.py
+++ b/solution.py
@@ -9,8 +9,8 @@
 
 TILE = 256
 AXIS = "device"
-VLIM = 28
-ROWS = 40
+VLIM = 40
+ROWS = 35
 F32 = jnp.float32
 BF16 = jnp.bfloat16
 HIGH = lax.Precision.HIGHEST
@@ -52,7 +52,7 @@
     return pl.BlockSpec(memory_space=pl.ANY)
 
 
-def pack_kernel(me_ref, q_hbm, p_hbm, c_hbm, out_ref, q_ref, p_ref, c_ref, sems):
+def pack_kernel(q_hbm, p_hbm, c_hbm, out_ref, q_ref, p_ref, c_ref, sems):
     pairs = [(q_hbm, q_ref), (p_hbm, p_ref), (c_hbm, c_ref)]
     arrivals = [pltpu.make_async_copy(src, dst, sems.at[i]) for i, (src, dst) in enumerate(pairs)]
     for copy in arrivals:
@@ -67,74 +67,48 @@
     cands = c_ref[...].astype(F32)
     rows.append(jnp.concatenate([cands[0:1, :], cands[1:2, :]], axis=1))
     rows.append(jnp.concatenate([cands[2:3, :], cands[3:4, :]], axis=1))
-    rows.append(jnp.full((ROWS - len(rows), 128), me_ref[0], jnp.int32).astype(F32))
     packet = jnp.concatenate(rows, axis=0)
-    for i in range(out_ref.shape[0]):
-        out_ref[i] = packet
-
-
-def pack(me, queries, probes, candidates, copies):
+    for i in range(out_ref.shape[0] // ROWS):
+        out_ref[i * ROWS : (i + 1) * ROWS, :] = packet
+
+
+def pack(queries, probes, candidates, copies):
     return pl.pallas_call(
         pack_kernel,
-        out_shape=jax.ShapeDtypeStruct((copies, ROWS, 128), F32),
-        in_specs=[smem()] + [hbm()] * 3,
+        out_shape=jax.ShapeDtypeStruct((copies * ROWS, 128), F32),
+        in_specs=[hbm()] * 3,
         out_specs=vmem(),
         scratch_shapes=[pltpu.VMEM(x.shape, x.dtype) for x in (queries, probes, candidates)]
         + [pltpu.SemaphoreType.DMA((3,))],
         compiler_params=pltpu.CompilerParams(vmem_limit_bytes=8 * 1024 * 1024),
-    )(me, *[in_hbm(x) for x in (queries, probes, candidates)])
-
-
-def fetch_kernel(have_ref, vecs_ref, have_out, vecs_out, sems):
-    copies = [
-        pltpu.make_async_copy(
-            vecs_ref.at[:, pl.ds(c * 128, 128)], vecs_out.at[:, c, :], sems.at[c]
-        )
-        for c in range(8)
-    ]
-    for copy in copies:
-        copy.start()
-    have_out[...] = have_ref[...]
-    for copy in copies:
-        copy.wait()
-
-
-def fetch(have, vectors):
-    return pl.pallas_call(
-        fetch_kernel,
-        out_shape=(
-            jax.ShapeDtypeStruct(have.shape, F32),
-            pltpu.VMEM((vectors.shape[0], 8, 128), F32),
-        ),
-        in_specs=[vmem(), hbm()],
-        out_specs=(vmem(), vmem()),
-        scratch_shapes=[pltpu.SemaphoreType.DMA((8,))],
-        compiler_params=pltpu.CompilerParams(vmem_limit_bytes=2 * 1024 * 1024),
-        cost_estimate=pl.CostEstimate(
-            flops=0, transcendentals=0, bytes_accessed=2 * vectors.size * 4
-        ),
-    )(have, in_hbm(vectors))
+    )(*[in_hbm(x) for x in (queries, probes, candidates)])
 
 
 def score_kernel(me_ref, *refs, n_blocks, n_lists, n_rows, v_dev):
     blocks = refs[:n_blocks]
-    tiles_hbm, scale_hbm, offset_hbm, vecs_ref, codes_hbm, out_ref = refs[n_blocks : n_blocks + 6]
+    tiles_hbm, scale_hbm, offset_hbm, vecs_hbm, codes_hbm, out_ref = refs[n_blocks : n_blocks + 6]
     (
-        tiles_ref, scale_ref, offset_ref, codes_ref,
-        fold, base_acc, prod, spot_v, spot_s, sem, small_sems, code_sems,
+        tiles_ref, scale_ref, offset_ref, codes_ref, vecs_ref,
+        fold, base_acc, prod, spot_v, spot_s, sem, small_sems, vec_sems, code_sems,
     ) = refs[n_blocks + 6 :]
     me = me_ref[0]
     code_copies = [
         pltpu.make_async_copy(codes_hbm.at[l], codes_ref.at[l], code_sems.at[l])
         for l in range(n_lists)
     ]
+    vec_copies = [
+        pltpu.make_async_copy(
+            vecs_hbm.at[:, pl.ds(c * 128, 128)], vecs_ref.at[:, c, :], vec_sems.at[c]
+        )
+        for c in range(8)
+    ]
     small_copies = [
         pltpu.make_async_copy(src, dst, small_sems.at[i])
         for i, (src, dst) in enumerate(
             [(scale_hbm, scale_ref), (offset_hbm, offset_ref), (tiles_hbm, tiles_ref)]
         )
     ]
-    for copy in small_copies + code_copies[:1]:
+    for copy in small_copies + vec_copies + code_copies[:1]:
         copy.start()
     n_tiles = n_rows // TILE
     per = blocks[0].shape[0] // ROWS
@@ -142,6 +116,17 @@
 
     def rows_of(r):
         return jnp.concatenate([b[pl.ds(r, per, stride=ROWS), :] for b in blocks], axis=0)
+
+    core, mine_y, mine_z = me % 2, me // 2 % 4, me // 8 % 4
+    major, minor = iota((per, 128), 0) // 4, iota((per, 128), 0) % 4
+    names = []
+    for b in range(n_blocks):
+        step = SHIFTS[b % 4]
+        from_core = core if b < n_blocks // 2 else 1 - core
+        by_z = (major * 4 + (mine_z + 4 - step) % 4) * 4 + minor
+        by_y = (major * 4 + minor) * 4 + (mine_y + 4 - step) % 4
+        names.append(jnp.where(from_core == 0, by_z, by_y) * 2 + from_core)
+    ident = jnp.concatenate(names, axis=0)
 
     cand = jnp.concatenate([rows_of(33), rows_of(34)], axis=1).astype(jnp.int32)
     local_id = cand - me * v_dev
@@ -171,8 +156,7 @@
     )
     seg = (iota((128, 384), 0) // 32 == iota((128, 384), 1) // 128).astype(BF16)
     hits = dot(eq, seg)
-    ident = rows_of(35)
-    perm = (ident == iota((dev, 128), 1).astype(F32)).astype(BF16)
+    perm = (ident == iota((dev, 128), 1)).astype(F32).astype(BF16)
 
     for copy in small_copies:
         copy.wait()
@@ -203,13 +187,15 @@
                 base_acc[l, s * dev + r0 : s * dev + r0 + per, :] = acc[s]
 
     to_smem.wait()
+    for copy in vec_copies:
+        copy.wait()
     code_copies[3].start()
 
     def gather(part):
         for j in range(part * 4, part * 4 + 4):
             b = j // per
             for k in range(4):
-                row, q = spot_s[k, j], pl.multiple_of(spot_s[4 + k, j], 8)
+                row, q = spot_s[k, j], spot_s[4 + k, j]
                 to = (k * dev + j) * 8
                 prod[to : to + 8, :] = vecs_ref[row] * blocks[b][pl.ds(q, 8), :]
 
@@ -250,8 +236,7 @@
 def score(me, tile_counts, blocks, scale, offset, vectors, codes):
     n_lists, n_rows, width = codes.shape
     v_dev = vectors.shape[0]
-    per = blocks[0].shape[0]
-    blocks = [b.reshape(per * ROWS, 128) for b in blocks]
+    per = blocks[0].shape[0] // ROWS
     dev = per * len(blocks)
     body = functools.partial(
         score_kernel, n_blocks=len(blocks), n_lists=n_lists, n_rows=n_rows, v_dev=v_dev
@@ -259,13 +244,14 @@
     return pl.pallas_call(
         body,
         out_shape=jax.ShapeDtypeStruct((dev, 128), F32),
-        in_specs=[smem()] + [vmem()] * len(blocks) + [hbm()] * 3 + [vmem(), hbm()],
+        in_specs=[smem()] + [vmem()] * len(blocks) + [hbm()] * 5,
         out_specs=vmem(),
         scratch_shapes=[
             pltpu.SMEM(tile_counts.shape, jnp.int32),
             pltpu.VMEM(scale.shape, F32),
             pltpu.VMEM(offset.shape, F32),
             pltpu.VMEM(codes.shape, BF16),
+            pltpu.VMEM((v_dev, 8, 128), F32),
             pltpu.VMEM((n_lists, 2 * dev, width), BF16),
             pltpu.VMEM((n_lists, 2 * dev, 128), F32),
             pltpu.VMEM((4 * dev * 8, 128), F32),
@@ -273,11 +259,12 @@
             pltpu.SMEM((8, dev), jnp.int32),
             pltpu.SemaphoreType.DMA,
             pltpu.SemaphoreType.DMA((3,)),
+            pltpu.SemaphoreType.DMA((8,)),
             pltpu.SemaphoreType.DMA((n_lists,)),
         ],
         compiler_params=pltpu.CompilerParams(vmem_limit_bytes=VLIM * 1024 * 1024),
     )(
-        me, *blocks, *[in_hbm(x) for x in (tile_counts, scale, offset)], vectors, in_hbm(codes)
+        me, *blocks, *[in_hbm(x) for x in (tile_counts, scale, offset, vectors, codes)]
     )
 
 
@@ -374,18 +361,18 @@
 
 
 LAST = "zy"
+SHIFTS = (0, 1, 3, 2)
 
 
 def local(queries, probes, codes, scale, offset, tile_counts, raw_vectors, candidates):
     me = lax.axis_index(AXIS).astype(jnp.int32).reshape(1)
-    copies = pack(me, queries, probes, candidates, 16)
+    copies = pack(queries, probes, candidates, 16)
     have = lax.all_to_all(
-        copies, AXIS, split_axis=0, concat_axis=0, tiled=True, axis_index_groups=plane_groups(LAST)
-    )
-    blocks = [have] + [lax.ppermute(have, AXIS, shift_pairs(k, LAST)) for k in (1, 3, 2)]
-    ours, vecs_in = fetch(have, raw_vectors)
-    blocks = blocks + [lax.ppermute(b, AXIS, other_core()) for b in [ours] + blocks[1:]]
-    found = score(me, tile_counts, blocks, scale, offset, vecs_in, codes)
+        copies.reshape(16, 1, ROWS * 128), AXIS, split_axis=0, concat_axis=0, tiled=True, axis_index_groups=plane_groups(LAST)
+    ).reshape(16 * ROWS, 128)
+    blocks = [have] + [lax.ppermute(have, AXIS, shift_pairs(k, LAST)) for k in SHIFTS[1:]]
+    blocks = blocks + [lax.ppermute(b, AXIS, other_core()) for b in blocks]
+    found = score(me, tile_counts, blocks, scale, offset, raw_vectors, codes)
     devices = found.shape[0]
     back = lax.all_to_all(found.reshape(devices, 1, 128), AXIS, split_axis=0, concat_axis=0, tiled=True)
     hot, row = where_to_look(probes, candidates)

time: 59.8 us -> 59.5 us (level)
  starting transfers between devices: 17.8 us -> 19.2 us
  Pallas kernels: 13.4 us -> 12.3 us
    pallas_call x2 -> x1, Pallas kernels: 3.12 us -> 0.85 us  [pack(): pl.pallas_call(pack_kernel, out_shape=jax.ShapeDtypeStruct((copies * ROWS...]
    ppermute x4, starting transfers between devices: 7.66 us -> 9.33 us  [local(): blocks = blocks + [lax.ppermute(b, AXIS, other_core()) for b in blocks]]
    pallas_call x1, Pallas kernels: 9.24 us -> 10.3 us  [score(): pl.pallas_call(body, out_shape=jax.ShapeDtypeStruct((dev, 128), F32), in_...]
  transfers between devices with their start and end apart: 8 -> 8, of which waited for: 3 -> 3; matrix products, arithmetic and copies ran while one was open for 0% -> 0% of each run, Pallas kernels for 4% -> 0%
where the time goes in v4:
time: 59.5 us; the launch traced here: 59.2 us
  starting transfers between devices  19.2 us (32%)
  blocking collectives  15.8 us (27%)
  Pallas kernels  12.3 us (21%)
  waiting for transfers between devices  11.2 us (19%)
  between operations  0.7 us (1%)
    all_to_all x1, blocking collectives, local(): lax.all_to_all(copies.reshape(16, 1, ROWS * 128), AXIS, split_axis=0, con...  15.8 us
    pallas_call x1, Pallas kernels, score(): pl.pallas_call(body, out_shape=jax.ShapeDtypeStruct((dev, 128), F32), in_...  10.3 us
    ppermute x4, starting transfers between devices, local(): blocks = blocks + [lax.ppermute(b, AXIS, other_core()) for b in blocks]  9.33 us
    all_to_all x1, waiting for transfers between devices, local(): lax.all_to_all(found.reshape(devices, 1, 128), AXIS, split_axis=0, concat...  9.26 us
    all_to_all x1, starting transfers between devices, local(): lax.all_to_all(found.reshape(devices, 1, 128), AXIS, split_axis=0, concat...  5.63 us
    ppermute x3, starting transfers between devices, local(): lax.ppermute(have, AXIS, shift_pairs(k, LAST))  4.26 us
    ppermute x4, waiting for transfers between devices, local(): blocks = blocks + [lax.ppermute(b, AXIS, other_core()) for b in blocks]  1.19 us
  transfers between devices with their start and end apart: 8, of which 3 were waited for; matrix products, arithmetic and copies ran while one was open for 0% of the time, Pallas kernels for 0%

profile of v4, /device:TPU:1, one launch (start us, length us, event | category | flops | bytes accessed | tf_op | source)
XLA Modules:
  0.0 59.2 jit_solution(11123636190000408960)
XLA Ops:
  0.6 0.0 copy-start.1
  0.6 0.0 copy-start
  0.6 0.9 %shard_map.95 = f32[560,128]{1,0:T(8,128)S(1)} custom-call(f32[4,1024]{1,0:T(4,128)} %q_hbm.1, s32[4,32]{1,0:T(4,128)} %p_ref.1, s32[4,64]{1,0:T(4,128)} %c_ref.1), custom_call_target="tpu_custom_call" | custom-call | tf_op jit(solution)/shard_map/pallas_call | solution.py:76
  1.5 15.8 %all_to_all.10 = f32[16,1,4480]{2,1,0:T(1,128)S(1)} all-to-all(f32[16,1,4480]{2,1,0:T(1,128)S(1)} %bitcast.12), channel_id=1, replica_groups={{0,2,4,6,32,34,36,38,64,66,68,70,96,98,100,102},{8,10,12,14,40,42,44,46..., dimensions={0} | all-to-all | bytes 573440 | tf_op jit(solution)/shard_map/all_to_all | solution.py:370
  17.3 1.2 %collective-permute-start = (f32[560,128]{1,0:T(8,128)S(1)}, f32[560,128]{1,0:T(8,128)S(1)}, u32[]{:S(2)}, u32[]{:S(2)}) collective-permute-start(f32[560,128]{1,0:T(8,128)S(1)} %bitcast.7), channel_id=1, source_target_pairs={{0,8},{1,3},{2,10},{3,5},{4,12},{5,7},{6,14},{7,1},{8,16},{9,11},{... | collective-permute-start | bytes 860168 | tf_op jit(solution)/shard_map/ppermute | solution.py:373
  18.5 1.5 %collective-permute-start.1 = (f32[560,128]{1,0:T(8,128)S(1)}, f32[560,128]{1,0:T(8,128)S(1)}, u32[]{:S(2)}, u32[]{:S(2)}) collective-permute-start(f32[560,128]{1,0:T(8,128)S(1)} %bitcast.8), channel_id=1, source_target_pairs={{0,24},{1,7},{2,26},{3,1},{4,28},{5,3},{6,30},{7,5},{8,0},{9,15},{... | collective-permute-start | bytes 860168 | tf_op jit(solution)/shard_map/ppermute | solution.py:373
  20.0 1.6 %collective-permute-start.2 = (f32[560,128]{1,0:T(8,128)S(1)}, f32[560,128]{1,0:T(8,128)S(1)}, u32[]{:S(2)}, u32[]{:S(2)}) collective-permute-start(f32[560,128]{1,0:T(8,128)S(1)} %bitcast.9), channel_id=1, source_target_pairs={{0,16},{1,5},{2,18},{3,7},{4,20},{5,1},{6,22},{7,3},{8,24},{9,13},... | collective-permute-start | bytes 860168 | tf_op jit(solution)/shard_map/ppermute | solution.py:373
  21.6 3.2 %collective-permute-start.3 = (f32[560,128]{1,0:T(8,128)S(1)}, f32[560,128]{1,0:T(8,128)S(1)}, u32[]{:S(2)}, u32[]{:S(2)}) collective-permute-start(f32[560,128]{1,0:T(8,128)S(1)} %bitcast.10), channel_id=1, source_target_pairs={{0,1},{1,0},{2,3},{3,2},{4,5},{5,4},{6,7},{7,6},{8,9},{9,8},{10,11... | collective-permute-start | bytes 860168 | tf_op jit(solution)/shard_map/ppermute | solution.py:374
  24.8 0.0 collective-permute-done.refs_1_
  24.8 2.5 %collective-permute-start.4 = (f32[560,128]{1,0:T(8,128)S(1)}, f32[560,128]{1,0:T(8,128)S(1)}, u32[]{:S(2)}, u32[]{:S(2)}) collective-permute-start(f32[560,128]{1,0:T(8,128)S(1)} %collective-permute-done.refs_1_), channel_id=1, source_target_pairs={{0,1},{1,0},{2,3},{3,2},{4,5},{5,4},{6,7},{7,6},{8,9},{9,8},{10,11... | collective-permute-start | bytes 860168 | tf_op jit(solution)/shard_map/ppermute | solution.py:374
  27.3 0.0 collective-permute-done.1.refs_2_
  27.3 0.5 collective-permute-start.5
  27.8 0.7 %collective-permute-done.2.refs_3_ = f32[560,128]{1,0:T(8,128)S(1)} collective-permute-done((f32[560,128]{1,0:T(8,128)S(1)}, f32[560,128]{1,0:T(8,128)S(1)}, u32[]{:S(2)}, u32[]{:S(2)}) %collective-permute-start.2) | collective-permute-done | bytes 286752 | tf_op jit(solution)/shard_map/ppermute | solution.py:373
  28.5 3.2 %collective-permute-start.6 = (f32[560,128]{1,0:T(8,128)S(1)}, f32[560,128]{1,0:T(8,128)S(1)}, u32[]{:S(2)}, u32[]{:S(2)}) collective-permute-start(f32[560,128]{1,0:T(8,128)S(1)} %collective-permute-done.2.refs_3_), channel_id=1, source_target_pairs={{0,1},{1,0},{2,3},{3,2},{4,5},{5,4},{6,7},{7,6},{8,9},{9,8},{10,11... | collective-permute-start | bytes 860168 | tf_op jit(solution)/shard_map/ppermute | solution.py:374
  31.7 0.0 collective-permute-done.3.refs_4_
  31.7 0.0 collective-permute-done.4.refs_5_
  31.7 0.0 collective-permute-done.5.refs_6_
  31.7 1.2 %collective-permute-done.6.refs_7_ = f32[560,128]{1,0:T(8,128)S(1)} collective-permute-done((f32[560,128]{1,0:T(8,128)S(1)}, f32[560,128]{1,0:T(8,128)S(1)}, u32[]{:S(2)}, u32[]{:S(2)}) %collective-permute-start.6) | collective-permute-done | bytes 286752 | tf_op jit(solution)/shard_map/ppermute | solution.py:374
  32.9 10.3 %shard_map.96 = f32[128,128]{1,0:T(8,128)} custom-call(s32[1]{0:T(128)} %bitcast.me_ref, f32[560,128]{1,0:T(8,128)S(1)} %bitcast.11, f32[560,128]{1,0:T(8,128)S(1)} %collective-permute-done.refs_1_, f32[560,128]{1,0:T(8,128)S(1)} %collective-permute-done.1.refs_2_, f32[560,128]{1,0:T(8,128)S(1)} %collective-permute-done.2.refs_3_, ...), custom_call_target="tpu_custom_call" | custom-call | tf_op jit(solution)/shard_map/pallas_call | solution.py:244
  43.2 5.6 %all-to-all-start.1 = ((f32[128,1,128]{2,1,0:T(1,128)}), f32[128,1,128]{2,1,0:T(1,128)S(1)}, u32[]{:S(2)}, u32[]{:S(2)}) async-start(f32[128,1,128]{2,1,0:T(1,128)} %bitcast.4), calls=%async_computation.1 | async-start | bytes 131072 | tf_op jit(solution)/shard_map/all_to_all | solution.py:377
  48.8 0.0 copy-done.1
  48.9 0.0 copy-done
  48.9 0.2 shard_map.97
  49.1 9.3 %all-to-all-done.1 = f32[128,1,128]{2,1,0:T(1,128)S(1)} async-done(((f32[128,1,128]{2,1,0:T(1,128)}), f32[128,1,128]{2,1,0:T(1,128)S(1)}, u32[]{:S(2)}, u32[]{:S(2)}) %all-to-all-start.1) | async-done | bytes 65568 | tf_op jit(solution)/shard_map/all_to_all | solution.py:377
  58.3 0.9 %shard_map.98 = (f32[4,32]{1,0:T(4,128)}, f32[4,64]{1,0:T(4,128)}) custom-call(f32[128,128]{1,0:T(8,128)S(1)} %bitcast.13, bf16[128,384]{1,0:T(8,128)(2,1)S(1)} %get-tuple-element.4.hot_ref, s32[8,384]{1,0:T(8,128)S(1)} %get-tuple-element.5.row_ref), custom_call_target="tpu_custom_call" | custom-call | tf_op jit(solution)/shard_map/pallas_call | solution.py:321
Async XLA Ops:
  0.6 48.2 %copy-start.1 = (s32[4,64]{1,0:T(4,128)S(1)}, s32[4,64]{1,0:T(4,128)}, u32[]{:S(2)}) copy-start(s32[4,64]{1,0:T(4,128)} %c_ref.1) | copy-start | bytes 3076
  0.6 48.2 %copy-start = (s32[4,32]{1,0:T(4,128)S(1)}, s32[4,32]{1,0:T(4,128)}, u32[]{:S(2)}) copy-start(s32[4,32]{1,0:T(4,128)} %p_ref.1) | copy-start | bytes 1540
  17.3 7.4 %collective-permute-start = (f32[560,128]{1,0:T(8,128)S(1)}, f32[560,128]{1,0:T(8,128)S(1)}, u32[]{:S(2)}, u32[]{:S(2)}) collective-permute-start(f32[560,128]{1,0:T(8,128)S(1)} %bitcast.7), channel_id=1, source_target_pairs={{0,8},{1,3},{2,10},{3,5},{4,12},{5,7},{6,14},{7,1},{8,16},{9,11},{... | collective-permute-start | bytes 860168 | tf_op jit(solution)/shard_map/ppermute | solution.py:373
  18.5 8.8 %collective-permute-start.1 = (f32[560,128]{1,0:T(8,128)S(1)}, f32[560,128]{1,0:T(8,128)S(1)}, u32[]{:S(2)}, u32[]{:S(2)}) collective-permute-start(f32[560,128]{1,0:T(8,128)S(1)} %bitcast.8), channel_id=1, source_target_pairs={{0,24},{1,7},{2,26},{3,1},{4,28},{5,3},{6,30},{7,5},{8,0},{9,15},{... | collective-permute-start | bytes 860168 | tf_op jit(solution)/shard_map/ppermute | solution.py:373
  20.0 8.5 %collective-permute-start.2 = (f32[560,128]{1,0:T(8,128)S(1)}, f32[560,128]{1,0:T(8,128)S(1)}, u32[]{:S(2)}, u32[]{:S(2)}) collective-permute-start(f32[560,128]{1,0:T(8,128)S(1)} %bitcast.9), channel_id=1, source_target_pairs={{0,16},{1,5},{2,18},{3,7},{4,20},{5,1},{6,22},{7,3},{8,24},{9,13},... | collective-permute-start | bytes 860168 | tf_op jit(solution)/shard_map/ppermute | solution.py:373
  21.6 10.1 %collective-permute-start.3 = (f32[560,128]{1,0:T(8,128)S(1)}, f32[560,128]{1,0:T(8,128)S(1)}, u32[]{:S(2)}, u32[]{:S(2)}) collective-permute-start(f32[560,128]{1,0:T(8,128)S(1)} %bitcast.10), channel_id=1, source_target_pairs={{0,1},{1,0},{2,3},{3,2},{4,5},{5,4},{6,7},{7,6},{8,9},{9,8},{10,11... | collective-permute-start | bytes 860168 | tf_op jit(solution)/shard_map/ppermute | solution.py:374
  24.8 6.9 %collective-permute-start.4 = (f32[560,128]{1,0:T(8,128)S(1)}, f32[560,128]{1,0:T(8,128)S(1)}, u32[]{:S(2)}, u32[]{:S(2)}) collective-permute-start(f32[560,128]{1,0:T(8,128)S(1)} %collective-permute-done.refs_1_), channel_id=1, source_target_pairs={{0,1},{1,0},{2,3},{3,2},{4,5},{5,4},{6,7},{7,6},{8,9},{9,8},{10,11... | collective-permute-start | bytes 860168 | tf_op jit(solution)/shard_map/ppermute | solution.py:374
  27.3 4.4 %collective-permute-start.5 = (f32[560,128]{1,0:T(8,128)S(1)}, f32[560,128]{1,0:T(8,128)S(1)}, u32[]{:S(2)}, u32[]{:S(2)}) collective-permute-start(f32[560,128]{1,0:T(8,128)S(1)} %collective-permute-done.1.refs_2_), channel_id=1, source_target_pairs={{0,1},{1,0},{2,3},{3,2},{4,5},{5,4},{6,7},{7,6},{8,9},{9,8},{10,11... | collective-permute-start | bytes 860168 | tf_op jit(solution)/shard_map/ppermute | solution.py:374
  28.5 4.3 %collective-permute-start.6 = (f32[560,128]{1,0:T(8,128)S(1)}, f32[560,128]{1,0:T(8,128)S(1)}, u32[]{:S(2)}, u32[]{:S(2)}) collective-permute-start(f32[560,128]{1,0:T(8,128)S(1)} %collective-permute-done.2.refs_3_), channel_id=1, source_target_pairs={{0,1},{1,0},{2,3},{3,2},{4,5},{5,4},{6,7},{7,6},{8,9},{9,8},{10,11... | collective-permute-start | bytes 860168 | tf_op jit(solution)/shard_map/ppermute | solution.py:374
  43.2 15.1 %all-to-all-start.1 = ((f32[128,1,128]{2,1,0:T(1,128)}), f32[128,1,128]{2,1,0:T(1,128)S(1)}, u32[]{:S(2)}, u32[]{:S(2)}) async-start(f32[128,1,128]{2,1,0:T(1,128)} %bitcast.4), calls=%async_computation.1 | async-start | bytes 131072 | tf_op jit(solution)/shard_map/all_to_all | solution.py:377

commit v5 on v4

--- a/solution.py
+++ b/solution.py
@@ -108,7 +108,7 @@
             [(scale_hbm, scale_ref), (offset_hbm, offset_ref), (tiles_hbm, tiles_ref)]
         )
     ]
-    for copy in small_copies + vec_copies + code_copies[:1]:
+    for copy in small_copies + code_copies[:1]:
         copy.start()
     n_tiles = n_rows // TILE
     per = blocks[0].shape[0] // ROWS
@@ -160,7 +160,8 @@
 
     for copy in small_copies:
         copy.wait()
-    code_copies[1].start()
+    for copy in [code_copies[1]] + vec_copies:
+        copy.start()
     for b in range(n_blocks):
         r0 = b * per
         if b == 4:
@@ -187,8 +188,6 @@
                 base_acc[l, s * dev + r0 : s * dev + r0 + per, :] = acc[s]
 
     to_smem.wait()
-    for copy in vec_copies:
-        copy.wait()
     code_copies[3].start()
 
     def gather(part):
@@ -205,6 +204,9 @@
     for l in range(n_lists):
         folded = fold[l]
         code_copies[l].wait()
+        if l == n_lists // 2:
+            for copy in vec_copies:
+                copy.wait()
         best = None
         for t in range(n_tiles):
             s = dot(codes_ref[l, t * TILE : (t + 1) * TILE, :], folded, NT)
@@ -213,7 +215,8 @@
                 best = m
             else:
                 best = jnp.where(t < tiles_ref[l], jnp.maximum(best, m), best)
-            if (l * n_tiles + t + 1) * (dev // 4) // steps > done:
+            due = (2 * (l * n_tiles + t + 1) - steps) * (dev // 4) // steps
+            while done < due:
                 gather(done)
                 done += 1
         best = jnp.max(best, axis=0, keepdims=True)

time: 59.5 us -> 60.2 us (1.012)
  Pallas kernels: 12.3 us -> 13.1 us
    pallas_call x1, Pallas kernels: 10.3 us -> 11.1 us  [score(): pl.pallas_call(body, out_shape=jax.ShapeDtypeStruct((dev, 128), F32), in_...]
where the time goes in v5:
time: 60.2 us; the launch traced here: 60 us
  starting transfers between devices  19.2 us (32%)
  blocking collectives  15.8 us (26%)
  Pallas kernels  13.1 us (22%)
  waiting for transfers between devices  11.2 us (19%)
  between operations  0.7 us (1%)
    all_to_all x1, blocking collectives, local(): lax.all_to_all(copies.reshape(16, 1, ROWS * 128), AXIS, split_axis=0, con...  15.8 us
    pallas_call x1, Pallas kernels, score(): pl.pallas_call(body, out_shape=jax.ShapeDtypeStruct((dev, 128), F32), in_...  11.1 us
    ppermute x4, starting transfers between devices, local(): blocks = blocks + [lax.ppermute(b, AXIS, other_core()) for b in blocks]  9.33 us
    all_to_all x1, waiting for transfers between devices, local(): lax.all_to_all(found.reshape(devices, 1, 128), AXIS, split_axis=0, concat...  9.26 us
    all_to_all x1, starting transfers between devices, local(): lax.all_to_all(found.reshape(devices, 1, 128), AXIS, split_axis=0, concat...  5.63 us
    ppermute x3, starting transfers between devices, local(): lax.ppermute(have, AXIS, shift_pairs(k, LAST))  4.26 us
  transfers between devices with their start and end apart: 8, of which 3 were waited for; matrix products, arithmetic and copies ran while one was open for 0% of the time, Pallas kernels for 0%

profile of v5, /device:TPU:1, one launch (start us, length us, event | category | flops | bytes accessed | tf_op | source)
XLA Modules:
  0.0 60.0 jit_solution(3184316762358525888)
XLA Ops:
  0.6 0.0 copy-start.1
  0.6 0.0 copy-start
  0.6 0.9 %shard_map.95 = f32[560,128]{1,0:T(8,128)S(1)} custom-call(f32[4,1024]{1,0:T(4,128)} %q_hbm.1, s32[4,32]{1,0:T(4,128)} %p_ref.1, s32[4,64]{1,0:T(4,128)} %c_ref.1), custom_call_target="tpu_custom_call" | custom-call | tf_op jit(solution)/shard_map/pallas_call | solution.py:76
  1.5 15.8 %all_to_all.10 = f32[16,1,4480]{2,1,0:T(1,128)S(1)} all-to-all(f32[16,1,4480]{2,1,0:T(1,128)S(1)} %bitcast.12), channel_id=1, replica_groups={{0,2,4,6,32,34,36,38,64,66,68,70,96,98,100,102},{8,10,12,14,40,42,44,46..., dimensions={0} | all-to-all | bytes 573440 | tf_op jit(solution)/shard_map/all_to_all | solution.py:373
  17.3 1.2 %collective-permute-start = (f32[560,128]{1,0:T(8,128)S(1)}, f32[560,128]{1,0:T(8,128)S(1)}, u32[]{:S(2)}, u32[]{:S(2)}) collective-permute-start(f32[560,128]{1,0:T(8,128)S(1)} %bitcast.7), channel_id=1, source_target_pairs={{0,8},{1,3},{2,10},{3,5},{4,12},{5,7},{6,14},{7,1},{8,16},{9,11},{... | collective-permute-start | bytes 860168 | tf_op jit(solution)/shard_map/ppermute | solution.py:376
  18.5 1.5 %collective-permute-start.1 = (f32[560,128]{1,0:T(8,128)S(1)}, f32[560,128]{1,0:T(8,128)S(1)}, u32[]{:S(2)}, u32[]{:S(2)}) collective-permute-start(f32[560,128]{1,0:T(8,128)S(1)} %bitcast.8), channel_id=1, source_target_pairs={{0,24},{1,7},{2,26},{3,1},{4,28},{5,3},{6,30},{7,5},{8,0},{9,15},{... | collective-permute-start | bytes 860168 | tf_op jit(solution)/shard_map/ppermute | solution.py:376
  20.0 1.6 %collective-permute-start.2 = (f32[560,128]{1,0:T(8,128)S(1)}, f32[560,128]{1,0:T(8,128)S(1)}, u32[]{:S(2)}, u32[]{:S(2)}) collective-permute-start(f32[560,128]{1,0:T(8,128)S(1)} %bitcast.9), channel_id=1, source_target_pairs={{0,16},{1,5},{2,18},{3,7},{4,20},{5,1},{6,22},{7,3},{8,24},{9,13},... | collective-permute-start | bytes 860168 | tf_op jit(solution)/shard_map/ppermute | solution.py:376
  21.6 3.2 %collective-permute-start.3 = (f32[560,128]{1,0:T(8,128)S(1)}, f32[560,128]{1,0:T(8,128)S(1)}, u32[]{:S(2)}, u32[]{:S(2)}) collective-permute-start(f32[560,128]{1,0:T(8,128)S(1)} %bitcast.10), channel_id=1, source_target_pairs={{0,1},{1,0},{2,3},{3,2},{4,5},{5,4},{6,7},{7,6},{8,9},{9,8},{10,11... | collective-permute-start | bytes 860168 | tf_op jit(solution)/shard_map/ppermute | solution.py:377
  24.8 0.0 collective-permute-done.refs_1_
  24.8 2.5 %collective-permute-start.4 = (f32[560,128]{1,0:T(8,128)S(1)}, f32[560,128]{1,0:T(8,128)S(1)}, u32[]{:S(2)}, u32[]{:S(2)}) collective-permute-start(f32[560,128]{1,0:T(8,128)S(1)} %collective-permute-done.refs_1_), channel_id=1, source_target_pairs={{0,1},{1,0},{2,3},{3,2},{4,5},{5,4},{6,7},{7,6},{8,9},{9,8},{10,11... | collective-permute-start | bytes 860168 | tf_op jit(solution)/shard_map/ppermute | solution.py:377
  27.3 0.0 collective-permute-done.1.refs_2_
  27.3 0.5 collective-permute-start.5
  27.8 0.7 %collective-permute-done.2.refs_3_ = f32[560,128]{1,0:T(8,128)S(1)} collective-permute-done((f32[560,128]{1,0:T(8,128)S(1)}, f32[560,128]{1,0:T(8,128)S(1)}, u32[]{:S(2)}, u32[]{:S(2)}) %collective-permute-start.2) | collective-permute-done | bytes 286752 | tf_op jit(solution)/shard_map/ppermute | solution.py:376
  28.5 3.2 %collective-permute-start.6 = (f32[560,128]{1,0:T(8,128)S(1)}, f32[560,128]{1,0:T(8,128)S(1)}, u32[]{:S(2)}, u32[]{:S(2)}) collective-permute-start(f32[560,128]{1,0:T(8,128)S(1)} %collective-permute-done.2.refs_3_), channel_id=1, source_target_pairs={{0,1},{1,0},{2,3},{3,2},{4,5},{5,4},{6,7},{7,6},{8,9},{9,8},{10,11... | collective-permute-start | bytes 860168 | tf_op jit(solution)/shard_map/ppermute | solution.py:377
  31.7 0.0 collective-permute-done.3.refs_4_
  31.7 0.0 collective-permute-done.4.refs_5_
  31.7 0.0 collective-permute-done.5.refs_6_
  31.7 1.2 %collective-permute-done.6.refs_7_ = f32[560,128]{1,0:T(8,128)S(1)} collective-permute-done((f32[560,128]{1,0:T(8,128)S(1)}, f32[560,128]{1,0:T(8,128)S(1)}, u32[]{:S(2)}, u32[]{:S(2)}) %collective-permute-start.6) | collective-permute-done | bytes 286752 | tf_op jit(solution)/shard_map/ppermute | solution.py:377
  32.9 11.1 %shard_map.96 = f32[128,128]{1,0:T(8,128)} custom-call(s32[1]{0:T(128)} %bitcast.me_ref, f32[560,128]{1,0:T(8,128)S(1)} %bitcast.11, f32[560,128]{1,0:T(8,128)S(1)} %collective-permute-done.refs_1_, f32[560,128]{1,0:T(8,128)S(1)} %collective-permute-done.1.refs_2_, f32[560,128]{1,0:T(8,128)S(1)} %collective-permute-done.2.refs_3_, ...), custom_call_target="tpu_custom_call" | custom-call | tf_op jit(solution)/shard_map/pallas_call | solution.py:247
  44.0 5.6 %all-to-all-start.1 = ((f32[128,1,128]{2,1,0:T(1,128)}), f32[128,1,128]{2,1,0:T(1,128)S(1)}, u32[]{:S(2)}, u32[]{:S(2)}) async-start(f32[128,1,128]{2,1,0:T(1,128)} %bitcast.4), calls=%async_computation.1 | async-start | bytes 131072 | tf_op jit(solution)/shard_map/all_to_all | solution.py:380
  49.6 0.0 copy-done.1
  49.7 0.0 copy-done
  49.7 0.2 shard_map.97
  49.9 9.3 %all-to-all-done.1 = f32[128,1,128]{2,1,0:T(1,128)S(1)} async-done(((f32[128,1,128]{2,1,0:T(1,128)}), f32[128,1,128]{2,1,0:T(1,128)S(1)}, u32[]{:S(2)}, u32[]{:S(2)}) %all-to-all-start.1) | async-done | bytes 65568 | tf_op jit(solution)/shard_map/all_to_all | solution.py:380
  59.1 0.9 %shard_map.98 = (f32[4,32]{1,0:T(4,128)}, f32[4,64]{1,0:T(4,128)}) custom-call(f32[128,128]{1,0:T(8,128)S(1)} %bitcast.13, bf16[128,384]{1,0:T(8,128)(2,1)S(1)} %get-tuple-element.4.hot_ref, s32[8,384]{1,0:T(8,128)S(1)} %get-tuple-element.5.row_ref), custom_call_target="tpu_custom_call" | custom-call | tf_op jit(solution)/shard_map/pallas_call | solution.py:324
Async XLA Ops:
  0.6 49.0 %copy-start.1 = (s32[4,64]{1,0:T(4,128)S(1)}, s32[4,64]{1,0:T(4,128)}, u32[]{:S(2)}) copy-start(s32[4,64]{1,0:T(4,128)} %c_ref.1) | copy-start | bytes 3076
  0.6 49.0 %copy-start = (s32[4,32]{1,0:T(4,128)S(1)}, s32[4,32]{1,0:T(4,128)}, u32[]{:S(2)}) copy-start(s32[4,32]{1,0:T(4,128)} %p_ref.1) | copy-start | bytes 1540
  17.3 7.4 %collective-permute-start = (f32[560,128]{1,0:T(8,128)S(1)}, f32[560,128]{1,0:T(8,128)S(1)}, u32[]{:S(2)}, u32[]{:S(2)}) collective-permute-start(f32[560,128]{1,0:T(8,128)S(1)} %bitcast.7), channel_id=1, source_target_pairs={{0,8},{1,3},{2,10},{3,5},{4,12},{5,7},{6,14},{7,1},{8,16},{9,11},{... | collective-permute-start | bytes 860168 | tf_op jit(solution)/shard_map/ppermute | solution.py:376
  18.5 8.8 %collective-permute-start.1 = (f32[560,128]{1,0:T(8,128)S(1)}, f32[560,128]{1,0:T(8,128)S(1)}, u32[]{:S(2)}, u32[]{:S(2)}) collective-permute-start(f32[560,128]{1,0:T(8,128)S(1)} %bitcast.8), channel_id=1, source_target_pairs={{0,24},{1,7},{2,26},{3,1},{4,28},{5,3},{6,30},{7,5},{8,0},{9,15},{... | collective-permute-start | bytes 860168 | tf_op jit(solution)/shard_map/ppermute | solution.py:376
  20.0 8.5 %collective-permute-start.2 = (f32[560,128]{1,0:T(8,128)S(1)}, f32[560,128]{1,0:T(8,128)S(1)}, u32[]{:S(2)}, u32[]{:S(2)}) collective-permute-start(f32[560,128]{1,0:T(8,128)S(1)} %bitcast.9), channel_id=1, source_target_pairs={{0,16},{1,5},{2,18},{3,7},{4,20},{5,1},{6,22},{7,3},{8,24},{9,13},... | collective-permute-start | bytes 860168 | tf_op jit(solution)/shard_map/ppermute | solution.py:376
  21.6 10.1 %collective-permute-start.3 = (f32[560,128]{1,0:T(8,128)S(1)}, f32[560,128]{1,0:T(8,128)S(1)}, u32[]{:S(2)}, u32[]{:S(2)}) collective-permute-start(f32[560,128]{1,0:T(8,128)S(1)} %bitcast.10), channel_id=1, source_target_pairs={{0,1},{1,0},{2,3},{3,2},{4,5},{5,4},{6,7},{7,6},{8,9},{9,8},{10,11... | collective-permute-start | bytes 860168 | tf_op jit(solution)/shard_map/ppermute | solution.py:377
  24.8 6.9 %collective-permute-start.4 = (f32[560,128]{1,0:T(8,128)S(1)}, f32[560,128]{1,0:T(8,128)S(1)}, u32[]{:S(2)}, u32[]{:S(2)}) collective-permute-start(f32[560,128]{1,0:T(8,128)S(1)} %collective-permute-done.refs_1_), channel_id=1, source_target_pairs={{0,1},{1,0},{2,3},{3,2},{4,5},{5,4},{6,7},{7,6},{8,9},{9,8},{10,11... | collective-permute-start | bytes 860168 | tf_op jit(solution)/shard_map/ppermute | solution.py:377
  27.3 4.4 %collective-permute-start.5 = (f32[560,128]{1,0:T(8,128)S(1)}, f32[560,128]{1,0:T(8,128)S(1)}, u32[]{:S(2)}, u32[]{:S(2)}) collective-permute-start(f32[560,128]{1,0:T(8,128)S(1)} %collective-permute-done.1.refs_2_), channel_id=1, source_target_pairs={{0,1},{1,0},{2,3},{3,2},{4,5},{5,4},{6,7},{7,6},{8,9},{9,8},{10,11... | collective-permute-start | bytes 860168 | tf_op jit(solution)/shard_map/ppermute | solution.py:377
  28.5 4.3 %collective-permute-start.6 = (f32[560,128]{1,0:T(8,128)S(1)}, f32[560,128]{1,0:T(8,128)S(1)}, u32[]{:S(2)}, u32[]{:S(2)}) collective-permute-start(f32[560,128]{1,0:T(8,128)S(1)} %collective-permute-done.2.refs_3_), channel_id=1, source_target_pairs={{0,1},{1,0},{2,3},{3,2},{4,5},{5,4},{6,7},{7,6},{8,9},{9,8},{10,11... | collective-permute-start | bytes 860168 | tf_op jit(solution)/shard_map/ppermute | solution.py:377
  44.0 15.1 %all-to-all-start.1 = ((f32[128,1,128]{2,1,0:T(1,128)}), f32[128,1,128]{2,1,0:T(1,128)S(1)}, u32[]{:S(2)}, u32[]{:S(2)}) async-start(f32[128,1,128]{2,1,0:T(1,128)} %bitcast.4), calls=%async_computation.1 | async-start | bytes 131072 | tf_op jit(solution)/shard_map/all_to_all | solution.py:380
